TPU v7x, 32 devices: a whole 2x2x4 slice. The times are simulated.
32 devices in a mesh: wide: 8 (over y, x, core), narrow: 4 (over z).
Axes of the slice: x: 2, y: 2, z: 4, core: 2. Of those that a mesh axis runs over, the one named last changes fastest.
Arguments:
- x_input: float32 [8, 1024, 1152], P('wide', 'narrow'), may hold values from -6 to 6
- condition: float32 [8, 1152], P('wide'), may hold values from -6 to 6
- counts: int32 [8], P('wide'), may hold values from 1 to 1, as said below
- w_ada: bfloat16 [1152, 6912], P(None, 'narrow'), may hold values from -0.1875 to 0.1875
- b_ada: bfloat16 [6912], P('narrow'), may hold values from -3 to 3
- w_qkv: bfloat16 [1152, 3456], P('narrow'), may hold values from -0.1875 to 0.1875
- qv_bias: bfloat16 [2304], P('narrow'), may hold values from -3 to 3
- w_out: bfloat16 [1152, 1152], P('narrow'), may hold values from -1.5 to 1.5
- b_out: bfloat16 [1152], P('narrow'), may hold values from -3 to 3
- w_fc1: bfloat16 [1152, 4608], P('narrow'), may hold values from -0.1875 to 0.1875
- b_fc1: bfloat16 [4608], P('narrow'), may hold values from -3 to 3
- w_fc2: bfloat16 [4608, 1152], P('narrow'), may hold values from -0.09375 to 0.09375
- b_fc2: bfloat16 [1152], P('narrow'), may hold values from -3 to 3
- d_out: float32 [8, 1024, 1152], P('wide', 'narrow'), may hold values from -6 to 6
Outputs:
- result: float32 [8, 1024, 1152], P('wide', 'narrow')
- grad_input: float32 [8, 1024, 1152], P('wide', 'narrow')
- grad_condition: float32 [8, 1152], P('wide')
- grad_w_ada: float32 [1152, 6912], P(None, 'narrow')
- grad_b_ada: float32 [6912], P('narrow')
- grad_w_qkv: float32 [1152, 3456], P('narrow')
- grad_qv_bias: float32 [2304], P('narrow')
- grad_w_out: float32 [1152, 1152], P('narrow')
- grad_b_out: float32 [1152], P('narrow')
- grad_w_fc1: float32 [1152, 4608], P('narrow')
- grad_b_fc1: float32 [4608], P('narrow')
- grad_w_fc2: float32 [4608, 1152], P('narrow')
- grad_b_fc2: float32 [1152], P('narrow')
Inputs may be any that keep to these rules, and one draw needn't show every extreme that they name: `counts`: each group holds 1 to 1 images, in its first slots; some group holds 1.
All inputs are finite; a program needn't handle non-finite values.
Results may differ from a plain program's by a relative error of at most 0.019.
Values may be sent and summed in bfloat16 or wider, within the bound.
No kernel may reach another device: no remote copies, remote signals or barrier semaphores. Data moves between devices by JAX's collectives and lax.ppermute only.
A program may use at most 256 MiB of HBM per device.

v0:
```python
import jax
import jax.numpy as jnp
from jax import lax
from jax.sharding import PartitionSpec as P

HEADS = 16


def normalize(rows_in):
    centered = rows_in - jnp.mean(rows_in, axis=-1, keepdims=True)
    return centered * lax.rsqrt(jnp.mean(centered * centered, axis=-1, keepdims=True) + 1e-06)


def modulate(rows_in, scale_part, shift_part):
    return normalize(rows_in) * (1.0 + scale_part) + shift_part


def gelu_tanh(values_in):
    return jax.nn.gelu(values_in, approximate=True)


def outer_sum(left_rows, right_rows):
    return jnp.einsum("rd,re->de", left_rows, right_rows, preferred_element_type=jnp.float32)


def column_sum(rows_in):
    return jnp.sum(rows_in.astype(jnp.float32), axis=0)


def per_device(
    x_input,
    condition,
    counts,
    w_ada,
    b_ada,
    w_qkv,
    qv_bias,
    w_out,
    b_out,
    w_fc1,
    b_fc1,
    w_fc2,
    b_fc2,
    d_out,
):
    slot_count, tok_dev, model_width = x_input.shape
    head_count = HEADS
    head_size = model_width // head_count
    score_scale = head_size ** (-0.5)
    row_count = slot_count * tok_dev
    living = (jnp.arange(slot_count) < counts[0]).astype(jnp.float32)[:, None, None]
    cond_act, silu_pull = jax.vjp(jax.nn.silu, condition)
    cond_low = cond_act.astype(jnp.bfloat16)
    mod_part = jnp.dot(cond_low, w_ada, preferred_element_type=jnp.float32) + b_ada.astype(
        jnp.float32
    )
    modulation = lax.all_gather(mod_part, "narrow", axis=1, tiled=True)
    shift_one, scale_one, gate_one, shift_two, scale_two, gate_two = [
        modulation[:, None, piece_index * model_width : (piece_index + 1) * model_width]
        for piece_index in range(6)
    ]
    gathered = (
        lax.all_gather(w_qkv, "narrow", axis=0, tiled=True),
        lax.all_gather(w_out, "narrow", axis=0, tiled=True),
        lax.all_gather(w_fc1, "narrow", axis=0, tiled=True),
        lax.all_gather(w_fc2, "narrow", axis=0, tiled=True),
        lax.all_gather(qv_bias, "narrow", axis=0, tiled=True),
        lax.all_gather(b_out, "narrow", axis=0, tiled=True),
        lax.all_gather(b_fc1, "narrow", axis=0, tiled=True),
        lax.all_gather(b_fc2, "narrow", axis=0, tiled=True),
    )
    qkv_full, out_full, fc1_full, fc2_full, qv_full, bout_full, bfc1_full, bfc2_full = gathered
    first_in, pull_one = jax.vjp(modulate, x_input, scale_one, shift_one)
    first_low = first_in.astype(jnp.bfloat16).reshape(row_count, model_width)
    qv_float = qv_full.astype(jnp.float32)
    bias_three = jnp.concatenate(
        [qv_float[:model_width], jnp.zeros((model_width,), jnp.float32), qv_float[model_width:]]
    )
    projected = (
        jnp.dot(first_low, qkv_full, preferred_element_type=jnp.float32) + bias_three
    ).astype(jnp.bfloat16)
    projected = projected.reshape(slot_count, tok_dev, 3 * model_width)
    query_flat = projected[:, :, :model_width]
    keys_local = projected[:, :, model_width : 2 * model_width]
    values_local = projected[:, :, 2 * model_width :]
    keys_all, values_all = (
        lax.all_gather(keys_local, "narrow", axis=1, tiled=True),
        lax.all_gather(values_local, "narrow", axis=1, tiled=True),
    )
    queries = query_flat.reshape(slot_count, tok_dev, head_count, head_size)
    keys_heads = keys_all.reshape(slot_count, -1, head_count, head_size)
    values_heads = values_all.reshape(slot_count, -1, head_count, head_size)

    def attend(slot_data):
        query_slot, key_slot, value_slot = slot_data
        scores = (
            jnp.einsum("qhd,khd->hqk", query_slot, key_slot, preferred_element_type=jnp.float32)
            * score_scale
        )
        row_max = jnp.max(scores, axis=-1, keepdims=True)
        exponent = jnp.exp(scores - row_max)
        row_total = jnp.sum(exponent, axis=-1, keepdims=True)
        attention = (exponent / row_total).astype(jnp.bfloat16)
        mixed_slot = jnp.einsum(
            "hqk,khd->qhd", attention, value_slot, preferred_element_type=jnp.float32
        )
        return (mixed_slot.astype(jnp.bfloat16), row_max[..., 0] + jnp.log(row_total[..., 0]))

    attended, log_total = lax.map(attend, (queries, keys_heads, values_heads))
    mixed_rows = attended.reshape(row_count, model_width)
    branch_one = (
        jnp.dot(mixed_rows, out_full, preferred_element_type=jnp.float32)
        + bout_full.astype(jnp.float32)
    ).reshape(slot_count, tok_dev, model_width)
    middle = x_input + gate_one * branch_one
    second_in, pull_two = jax.vjp(modulate, middle, scale_two, shift_two)
    second_low = second_in.astype(jnp.bfloat16).reshape(row_count, model_width)
    hidden_pre = jnp.dot(
        second_low, fc1_full, preferred_element_type=jnp.float32
    ) + bfc1_full.astype(jnp.float32)
    active_pre, gelu_pull = jax.vjp(gelu_tanh, hidden_pre)
    active_low = active_pre.astype(jnp.bfloat16)
    branch_two = (
        jnp.dot(active_low, fc2_full, preferred_element_type=jnp.float32)
        + bfc2_full.astype(jnp.float32)
    ).reshape(slot_count, tok_dev, model_width)
    result = living * (middle + gate_two * branch_two)
    weights_back = (
        lax.all_gather(w_qkv, "narrow", axis=0, tiled=True),
        lax.all_gather(w_out, "narrow", axis=0, tiled=True),
        lax.all_gather(w_fc1, "narrow", axis=0, tiled=True),
        lax.all_gather(w_fc2, "narrow", axis=0, tiled=True),
        lax.all_gather(qv_bias, "narrow", axis=0, tiled=True),
        lax.all_gather(b_out, "narrow", axis=0, tiled=True),
        lax.all_gather(b_fc1, "narrow", axis=0, tiled=True),
        lax.all_gather(b_fc2, "narrow", axis=0, tiled=True),
    )
    qkv_back, out_back, fc1_back, fc2_back = (
        weights_back[0],
        weights_back[1],
        weights_back[2],
        weights_back[3],
    )
    grad_out = living * d_out
    grad_two = (gate_two * grad_out).astype(jnp.bfloat16).reshape(row_count, model_width)
    grad_gate_two = jnp.sum(grad_out * branch_two, axis=1)
    grad_bfc2 = column_sum(grad_two)
    grad_wfc2 = outer_sum(active_low, grad_two)
    grad_active = jnp.dot(grad_two, fc2_back.T, preferred_element_type=jnp.float32)
    grad_hidden = gelu_pull(grad_active)[0].astype(jnp.bfloat16)
    grad_bfc1 = column_sum(grad_hidden)
    grad_wfc1 = outer_sum(second_low, grad_hidden)
    grad_second = jnp.dot(grad_hidden, fc1_back.T, preferred_element_type=jnp.float32).reshape(
        slot_count, tok_dev, model_width
    )
    grad_middle, grad_scale_two, grad_shift_two = pull_two(grad_second)
    grad_middle = grad_middle + grad_out
    grad_one = (gate_one * grad_middle).astype(jnp.bfloat16).reshape(row_count, model_width)
    grad_gate_one = jnp.sum(grad_middle * branch_one, axis=1)
    grad_bout = column_sum(grad_one)
    grad_wout = outer_sum(mixed_rows, grad_one)
    grad_mixed = jnp.dot(grad_one, out_back.T, preferred_element_type=jnp.float32).astype(
        jnp.bfloat16
    )
    grad_mixed_heads = grad_mixed.reshape(slot_count, tok_dev, head_count, head_size)

    def query_scores(query_slot, key_slot, value_slot, grad_slot, lse_slot):
        scores = (
            jnp.einsum("qhd,khd->hqk", query_slot, key_slot, preferred_element_type=jnp.float32)
            * score_scale
        )
        attention = jnp.exp(scores - lse_slot[..., None])
        grad_attention = jnp.einsum(
            "qhd,khd->hqk", grad_slot, value_slot, preferred_element_type=jnp.float32
        )
        row_delta = jnp.sum(attention * grad_attention, axis=-1, keepdims=True)
        grad_scores = (attention * (grad_attention - row_delta)).astype(jnp.bfloat16)
        grad_query = (
            jnp.einsum("hqk,khd->qhd", grad_scores, key_slot, preferred_element_type=jnp.float32)
            * score_scale
        )
        return (attention, grad_scores, grad_query, row_delta[..., 0])

    def full_side(slot_data):
        query_slot, key_slot, value_slot, grad_slot, lse_slot = slot_data
        attention, grad_scores, grad_query, row_delta = query_scores(
            query_slot, key_slot, value_slot, grad_slot, lse_slot
        )
        grad_key = (
            jnp.einsum("hqk,qhd->khd", grad_scores, query_slot, preferred_element_type=jnp.float32)
            * score_scale
        )
        grad_value = jnp.einsum(
            "hqk,qhd->khd",
            attention.astype(jnp.bfloat16),
            grad_slot,
            preferred_element_type=jnp.float32,
        )
        return (grad_query, grad_key, grad_value)

    grad_queries, key_part, value_part = lax.map(
        full_side, (queries, keys_heads, values_heads, grad_mixed_heads, log_total)
    )
    grad_keys, grad_values = (
        lax.psum_scatter(
            key_part.reshape(slot_count, -1, model_width).astype(jnp.bfloat16),
            "narrow",
            scatter_dimension=1,
            tiled=True,
        ).astype(jnp.float32),
        lax.psum_scatter(
            value_part.reshape(slot_count, -1, model_width).astype(jnp.bfloat16),
            "narrow",
            scatter_dimension=1,
            tiled=True,
        ).astype(jnp.float32),
    )
    grad_projected = (
        jnp.concatenate(
            [grad_queries.reshape(slot_count, tok_dev, model_width), grad_keys, grad_values],
            axis=-1,
        )
        .astype(jnp.bfloat16)
        .reshape(row_count, 3 * model_width)
    )
    grad_wqkv = outer_sum(first_low, grad_projected)
    projected_sums = column_sum(grad_projected)
    grad_qv = jnp.concatenate([projected_sums[:model_width], projected_sums[2 * model_width :]])
    grad_first = jnp.dot(grad_projected, qkv_back.T, preferred_element_type=jnp.float32).reshape(
        slot_count, tok_dev, model_width
    )
    grad_from_norm, grad_scale_one, grad_shift_one = pull_one(grad_first)
    grad_input = grad_from_norm + grad_middle
    mod_grad_part = jnp.concatenate(
        [
            grad_shift_one[:, 0],
            grad_scale_one[:, 0],
            grad_gate_one,
            grad_shift_two[:, 0],
            grad_scale_two[:, 0],
            grad_gate_two,
        ],
        axis=1,
    )
    mod_grad = lax.psum_scatter(mod_grad_part, "narrow", scatter_dimension=1, tiled=True)
    mod_grad_low = mod_grad.astype(jnp.bfloat16)
    grad_wada = outer_sum(cond_low, mod_grad_low)
    grad_bada = column_sum(mod_grad_low)
    cond_part = jnp.dot(mod_grad_low, w_ada.T, preferred_element_type=jnp.float32)
    cond_total = lax.psum(cond_part, "narrow")
    grad_condition = silu_pull(cond_total)[0]
    local_grads = (
        grad_wqkv,
        grad_wout,
        grad_wfc1,
        grad_wfc2,
        grad_qv,
        grad_bout,
        grad_bfc1,
        grad_bfc2,
    )
    shards = (
        lax.psum_scatter(
            local_grads[0].astype(jnp.bfloat16), "narrow", scatter_dimension=0, tiled=True
        ).astype(jnp.float32),
        lax.psum_scatter(
            local_grads[1].astype(jnp.bfloat16), "narrow", scatter_dimension=0, tiled=True
        ).astype(jnp.float32),
        lax.psum_scatter(
            local_grads[2].astype(jnp.bfloat16), "narrow", scatter_dimension=0, tiled=True
        ).astype(jnp.float32),
        lax.psum_scatter(
            local_grads[3].astype(jnp.bfloat16), "narrow", scatter_dimension=0, tiled=True
        ).astype(jnp.float32),
        lax.psum_scatter(
            local_grads[4].astype(jnp.bfloat16), "narrow", scatter_dimension=0, tiled=True
        ).astype(jnp.float32),
        lax.psum_scatter(
            local_grads[5].astype(jnp.bfloat16), "narrow", scatter_dimension=0, tiled=True
        ).astype(jnp.float32),
        lax.psum_scatter(
            local_grads[6].astype(jnp.bfloat16), "narrow", scatter_dimension=0, tiled=True
        ).astype(jnp.float32),
        lax.psum_scatter(
            local_grads[7].astype(jnp.bfloat16), "narrow", scatter_dimension=0, tiled=True
        ).astype(jnp.float32),
    )
    summed = (
        lax.psum(shards[0].astype(jnp.bfloat16), "wide").astype(jnp.float32),
        lax.psum(shards[1].astype(jnp.bfloat16), "wide").astype(jnp.float32),
        lax.psum(shards[2].astype(jnp.bfloat16), "wide").astype(jnp.float32),
        lax.psum(shards[3].astype(jnp.bfloat16), "wide").astype(jnp.float32),
        lax.psum(shards[4].astype(jnp.bfloat16), "wide").astype(jnp.float32),
        lax.psum(shards[5].astype(jnp.bfloat16), "wide").astype(jnp.float32),
        lax.psum(shards[6].astype(jnp.bfloat16), "wide").astype(jnp.float32),
        lax.psum(shards[7].astype(jnp.bfloat16), "wide").astype(jnp.float32),
        lax.psum(grad_wada.astype(jnp.bfloat16), "wide").astype(jnp.float32),
        lax.psum(grad_bada.astype(jnp.bfloat16), "wide").astype(jnp.float32),
    )
    owned = summed[:8]
    ada_w, ada_b = (summed[8], summed[9])
    return (
        result,
        grad_input,
        grad_condition,
        ada_w,
        ada_b,
        owned[0],
        owned[4],
        owned[1],
        owned[5],
        owned[2],
        owned[6],
        owned[3],
        owned[7],
    )


def solution(mesh):
    in_specs = (
        P("wide", "narrow", None),
        P("wide", None),
        P("wide"),
        P(None, "narrow"),
        P("narrow"),
        P("narrow", None),
        P("narrow"),
        P("narrow", None),
        P("narrow"),
        P("narrow", None),
        P("narrow"),
        P("narrow", None),
        P("narrow"),
        P("wide", "narrow", None),
    )
    out_specs = (
        P("wide", "narrow", None),
        P("wide", "narrow", None),
        P("wide", None),
        P(None, "narrow"),
        P("narrow"),
        P("narrow", None),
        P("narrow"),
        P("narrow", None),
        P("narrow"),
        P("narrow", None),
        P("narrow"),
        P("narrow", None),
        P("narrow"),
    )
    return jax.shard_map(
        per_device, mesh=mesh, in_specs=in_specs, out_specs=out_specs, check_vma=False
    )
```

profile of v0, /device:TPU:0, one launch (start us, length us, event | category | flops | bytes accessed | tf_op | source)
XLA Modules:
  0.0 1723.3 jit_solution(10232845884247845259)
XLA Ops:
  16.1 24.1 %all-reduce = f32[6912]{0:T(1024)S(1)} all-reduce(f32[6912]{0:T(1024)S(1)} %add_dynamic-update-slice_fusion), channel_id=2, replica_groups=mesh['wide'=8,'narrow'=4] {'narrow'}, use_global_device_ids=true, to_apply=%add | all-reduce | flops 6912 | bytes 55296
  40.9 21.1 %all-reduce.11 = (bf16[2304]{0:T(1024)(128)(2,1)S(1)}, bf16[1152]{0:T(1024)(128)(2,1)S(1)}) all-reduce(bf16[2304]{0:T(1024)(128)(2,1)S(1)} %dynamic-update-slice.1, bf16[1152]{0:T(1024)(128)(2,1)S(1)} %dynamic-update-slice.2), channel_id=1, replica_groups=mesh['wide'=8,'narrow'=4] {'narrow'}, use_global_device_ids=true, to_apply=%add.1 | all-reduce | flops 3456 | bytes 13824
  63.1 93.1 %all-gather.9.cloned.1.call-done = bf16[1152,3456]{1,0:T(8,128)(2,1)} async-done(((bf16[288,3456]{1,0:T(8,128)(2,1)}), bf16[1152,3456]{1,0:T(8,128)(2,1)}) %all-gather.9.cloned.1.call-update) | async-done | bytes 7962640 | tf_op jit(solution)/shard_map/all_gather | solution.py:63
  165.9 13.3 all-gather.1
  183.1 29.3 %all-gather.13.cloned.1.call-done = bf16[1,1024,1152]{2,1,0:T(8,128)(2,1)} async-done(((bf16[1,256,1152]{2,1,0:T(8,128)(2,1)}), bf16[1,1024,1152]{2,1,0:T(8,128)(2,1)}) %all-gather.13.cloned.1.call-update) | async-done | bytes 2359312 | tf_op jit(solution)/shard_map/all_gather | solution.py:87
  215.8 48.2 %all-gather.11.cloned.1.call-done = bf16[1,1024,1152]{2,1,0:T(8,128)(2,1)} async-done(((bf16[1,256,1152]{2,1,0:T(8,128)(2,1)}), bf16[1,1024,1152]{2,1,0:T(8,128)(2,1)}) %all-gather.11.cloned.1.call-update) | async-done | bytes 2359312 | tf_op jit(solution)/shard_map/all_gather | solution.py:88
  284.2 35.4 %all-gather.15.cloned.1.call-done = bf16[1152,1152]{1,0:T(8,128)(2,1)} async-done(((bf16[288,1152]{1,0:T(8,128)(2,1)}), bf16[1152,1152]{1,0:T(8,128)(2,1)}) %all-gather.15.cloned.1.call-update) | async-done | bytes 2654224 | tf_op jit(solution)/shard_map/all_gather | solution.py:64
  325.5 180.3 %all-gather.17.cloned.1.call-done = bf16[1152,4608]{1,0:T(8,128)(2,1)} async-done(((bf16[288,4608]{1,0:T(8,128)(2,1)}), bf16[1152,4608]{1,0:T(8,128)(2,1)}) %all-gather.17.cloned.1.call-update) | async-done | bytes 10616848 | tf_op jit(solution)/shard_map/all_gather | solution.py:65
  505.9 10.0 convolution_add_fusion
  515.9 175.7 %all-gather.19.cloned.1.call-done = bf16[4608,1152]{1,0:T(8,128)(2,1)} async-done(((bf16[1152,1152]{1,0:T(8,128)(2,1)}), bf16[4608,1152]{1,0:T(8,128)(2,1)}) %all-gather.19.cloned.1.call-update) | async-done | bytes 10616848 | tf_op jit(solution)/shard_map/all_gather | solution.py:66
  691.6 9.3 fusion.66
  702.3 8.0 fusion.22
  719.8 12.7 multiply_reduce_fusion
  732.5 12.0 multiply_convert_fusion
  748.5 10.9 fusion.16
  763.1 6.9 fusion.20
  770.1 24.8 %reduce-scatter.10.cloned.1.call-done = bf16[1,256,1152]{1,2,0:T(8,128)(2,1)} async-done(((bf16[1,1024,1152]{1,2,0:T(8,128)(2,1)}), bf16[1,256,1152]{1,2,0:T(8,128)(2,1)}) %reduce-scatter.10.cloned.1.call-update) | async-done | bytes 589840 | tf_op jit(solution)/shard_map/reduce_scatter | solution.py:205
  794.8 50.4 %reduce-scatter.12.cloned.1.call-done = bf16[1,256,1152]{1,2,0:T(8,128)(2,1)} async-done(((bf16[1,1024,1152]{1,2,0:T(8,128)(2,1)}), bf16[1,256,1152]{1,2,0:T(8,128)(2,1)}) %reduce-scatter.12.cloned.1.call-update) | async-done | bytes 589840 | tf_op jit(solution)/shard_map/reduce_scatter | solution.py:211
  847.8 8.1 fusion.24
  860.5 18.5 %all-reduce.10 = (bf16[1152]{0:T(1024)(128)(2,1)}, bf16[2304]{0:T(1024)(128)(2,1)}, bf16[1152]{0:T(1024)(128)(2,1)}, bf16[4608]{0:T(1024)(128)(2,1)}, bf16[1152]{0:T(1024)(128)(2,1)}) all-reduce(bf16[1152]{0:T(1024)(128)(2,1)} %copy-done.53, bf16[2304]{0:T(1024)(128)(2,1)} %pad_maximum_fusion.2, ...), channel_id=1, replica_groups=mesh['wide'=8,'narrow'=4] {'narrow'}, use_global_device_ids=true, to_apply=%add.3 | all-reduce | flops 10368 | bytes 41472
  884.9 10.0 fusion.21
  903.8 6.9 convolution_convert_fusion.2
  911.4 8.8 convolution_convert_fusion.1
  921.3 10.4 convolution_convert_fusion
  932.4 31.1 %reduce-scatter.22.cloned.1.call-done = f32[1728,1]{1,0:T(8,128)} async-done(((f32[6912,1]{1,0:T(8,128)}), f32[1728,1]{1,0:T(8,128)}) %reduce-scatter.22.cloned.1.call-update) | async-done | bytes 6928
  968.0 51.1 %reduce-scatter.16.cloned.1.call-done = bf16[288,1152]{1,0:T(8,128)(2,1)} async-done(((bf16[1152,1152]{1,0:T(8,128)(2,1)}), bf16[288,1152]{1,0:T(8,128)(2,1)}) %reduce-scatter.16.cloned.1.call-update) | async-done | bytes 663568 | tf_op jit(solution)/shard_map/reduce_scatter | solution.py:266
  1019.1 140.7 %reduce-scatter.14.cloned.1.call-done = bf16[288,3456]{1,0:T(8,128)(2,1)} async-done(((bf16[1152,3456]{1,0:T(8,128)(2,1)}), bf16[288,3456]{1,0:T(8,128)(2,1)}) %reduce-scatter.14.cloned.1.call-update) | async-done | bytes 1990672 | tf_op jit(solution)/shard_map/reduce_scatter | solution.py:263
  1159.9 183.1 %reduce-scatter.18.cloned.1.call-done = bf16[288,4608]{1,0:T(8,128)(2,1)} async-done(((bf16[1152,4608]{1,0:T(8,128)(2,1)}), bf16[288,4608]{1,0:T(8,128)(2,1)}) %reduce-scatter.18.cloned.1.call-update) | async-done | bytes 2654224 | tf_op jit(solution)/shard_map/reduce_scatter | solution.py:269
  1343.0 183.6 %reduce-scatter.20.cloned.1.call-done = bf16[1152,1152]{1,0:T(8,128)(2,1)} async-done(((bf16[4608,1152]{1,0:T(8,128)(2,1)}), bf16[1152,1152]{1,0:T(8,128)(2,1)}) %reduce-scatter.20.cloned.1.call-update) | async-done | bytes 2654224 | tf_op jit(solution)/shard_map/reduce_scatter | solution.py:272
  1536.8 25.9 %all-reduce.8 = (bf16[1728]{0:T(1024)(128)(2,1)S(1)}, bf16[576]{0:T(1024)(128)(2,1)S(1)}, bf16[288]{0:T(512)(128)(2,1)S(1)}, bf16[1152]{0:T(1024)(128)(2,1)S(1)}, bf16[288]{0:T(512)(128)(2,1)S(1)}) all-reduce(bf16[1728]{0:T(1024)(128)(2,1)S(1)} %copy-done.44, ...), channel_id=1, replica_groups=mesh['wide'=8,'narrow'=4] {'wide'}, use_global_device_ids=true, to_apply=%region_22.23 | all-reduce | flops 4032 | bytes 16128 | tf_op jit(solution)/shard_map/psum | solution.py:298
  1568.6 11.8 psum.77
  1581.0 120.4 %all-reduce.14.cloned.1.call-done = (bf16[1152,1728]{0,1:T(8,128)(2,1)}, bf16[288,3456]{1,0:T(8,128)(2,1)}, bf16[288,1152]{1,0:T(8,128)(2,1)}, bf16[288,4608]{1,0:T(8,128)(2,1)}, bf16[1152,1152]{1,0:T(8,128)(2,1)}) async-done(((bf16[1152,1728]{0,1:T(8,128)(2,1)}, bf16[288,3456]{1,0:T(8,128)(2,1)}, bf16[288,1152]{1,0:T(8,128)(2,1)}, bf16[288,4608]{1,0:T(8,128)(2,1)}, bf16[1152,1152]{1,0:T(8,128)(2,1)}), ...) | async-done | bytes 11943952 | tf_op jit(solution)/shard_map/psum | solution.py:297
  (247 shorter events, 128.3 us)
Async XLA Ops:
  7.2 33.1 %copy-start.2 = (f32[1,256,1152]{2,1,0:T(8,128)S(1)}, f32[1,256,1152]{2,1,0:T(8,128)}, u32[]{:S(2)}) copy-start(f32[1,256,1152]{2,1,0:T(8,128)} %param.14) | copy-start | bytes 3538948
  7.2 148.9 %all-gather.9.cloned.1.call-start = ((), (), s32[]{:S(2)}) async-start(), calls=%async_computation.7 | async-start | bytes 9953280 | tf_op jit(solution)/shard_map/all_gather | solution.py:63
  7.9 204.5 %all-gather.13.cloned.1.call-start = ((), (), s32[]{:S(2)}) async-start(), calls=%async_computation.9 | async-start | bytes 2949120 | tf_op jit(solution)/shard_map/all_gather | solution.py:87
  12.6 27.8 %copy-start.66 = (bf16[288]{0:T(512)(128)(2,1)S(1)}, bf16[288]{0:T(512)(128)(2,1)}, u32[]{:S(2)}) copy-start(bf16[288]{0:T(512)(128)(2,1)} %param.22) | copy-start | bytes 1732
  12.6 28.1 %copy-start.65 = (bf16[576]{0:T(1024)(128)(2,1)S(1)}, bf16[576]{0:T(1024)(128)(2,1)}, u32[]{:S(2)}) copy-start(bf16[576]{0:T(1024)(128)(2,1)} %param.20) | copy-start | bytes 3460
  62.7 99.3 %copy-start.29 = (f32[1152]{0:T(1024)}, f32[1152]{0:T(1024)S(1)}, u32[]{:S(2)}) copy-start(f32[1152]{0:T(1024)S(1)} %get-tuple-element.66) | copy-start | bytes 13828
  62.7 99.3 %copy-start.33 = (f32[1152]{0:T(1024)}, f32[1152]{0:T(1024)S(1)}, u32[]{:S(2)}) copy-start(f32[1152]{0:T(1024)S(1)} %get-tuple-element.65) | copy-start | bytes 13828
  62.7 117.7 %copy-start.45 = (f32[1152]{0:T(1024)}, f32[1152]{0:T(1024)S(1)}, u32[]{:S(2)}) copy-start(f32[1152]{0:T(1024)S(1)} %get-tuple-element.62) | copy-start | bytes 13828
  62.7 256.8 %copy-start.35 = (f32[1152]{0:T(1024)}, f32[1152]{0:T(1024)S(1)}, u32[]{:S(2)}) copy-start(f32[1152]{0:T(1024)S(1)} %get-tuple-element.67) | copy-start | bytes 13828
  62.8 99.3 %copy-start.50 = (f32[256]{0:T(256)}, f32[256]{0:T(256)S(1)}, u32[]{:S(2)}) copy-start(f32[256]{0:T(256)S(1)} %broadcast_multiply_fusion.1) | copy-start | bytes 3076
  63.0 99.1 %copy-start.57 = (f32[256]{0:T(256)}, f32[256]{0:T(256)S(1)}, u32[]{:S(2)}) copy-start(f32[256]{0:T(256)S(1)} %multiply_reduce_fusion.3) | copy-start | bytes 3076
  63.0 99.1 %copy-start.56 = (f32[256]{0:T(256)}, f32[256]{0:T(256)S(1)}, u32[]{:S(2)}) copy-start(f32[256]{0:T(256)S(1)} %fusion.46) | copy-start | bytes 3076
  163.3 100.7 %all-gather.11.cloned.1.call-start = ((), (), s32[]{:S(2)}) async-start(), calls=%async_computation.8 | async-start | bytes 2949120 | tf_op jit(solution)/shard_map/all_gather | solution.py:88
  164.0 155.6 %all-gather.15.cloned.1.call-start = ((), (), s32[]{:S(2)}) async-start(), calls=%async_computation.10 | async-start | bytes 3317760 | tf_op jit(solution)/shard_map/all_gather | solution.py:64
  164.6 15.9 copy-start.10
  164.6 341.2 %all-gather.17.cloned.1.call-start = ((), (), s32[]{:S(2)}) async-start(), calls=%async_computation.11 | async-start | bytes 13271040 | tf_op jit(solution)/shard_map/all_gather | solution.py:65
  165.2 526.4 %all-gather.19.cloned.1.call-start = ((), (), s32[]{:S(2)}) async-start(), calls=%async_computation.12 | async-start | bytes 13271040 | tf_op jit(solution)/shard_map/all_gather | solution.py:66
  165.8 629.0 %reduce-scatter.10.cloned.1.call-start = ((), (), s32[]{:S(2)}) async-start(), calls=%async_computation.13 | async-start | bytes 2949120 | tf_op jit(solution)/shard_map/reduce_scatter | solution.py:205
  732.5 12.0 copy-start.8
  748.4 96.8 %reduce-scatter.12.cloned.1.call-start = ((), (), s32[]{:S(2)}) async-start(), calls=%async_computation.14 | async-start | bytes 2949120 | tf_op jit(solution)/shard_map/reduce_scatter | solution.py:211
  759.4 204.1 %reduce-scatter.22.cloned.1.call-start = ((), (), s32[]{:S(2)}) async-start(), calls=%async_computation.19 | async-start | bytes 4423680
  763.1 84.7 %copy-start.30 = (f32[1152]{0:T(1024)S(1)}, f32[1152]{0:T(1024)}, u32[]{:S(2)}) copy-start(f32[1152]{0:T(1024)} %copy-done.29) | copy-start | bytes 13828
  847.8 37.0 %copy-start.5 = (f32[1,256,1152]{2,1,0:T(8,128)S(1)}, f32[1,256,1152]{2,1,0:T(8,128)}, u32[]{:S(2)}) copy-start(f32[1,256,1152]{2,1,0:T(8,128)} %copy-done.3) | copy-start | bytes 3538948
  847.8 37.0 %copy-start.12 = (f32[1,256,1152]{2,1,0:T(8,128)S(1)}, f32[1,256,1152]{2,1,0:T(8,128)}, u32[]{:S(2)}) copy-start(f32[1,256,1152]{2,1,0:T(8,128)} %param.27) | copy-start | bytes 3538948
  847.8 37.0 %copy-start.46 = (f32[1152]{0:T(1024)S(1)}, f32[1152]{0:T(1024)}, u32[]{:S(2)}) copy-start(f32[1152]{0:T(1024)} %copy-done.45) | copy-start | bytes 13828
  898.6 120.6 %reduce-scatter.16.cloned.1.call-start = ((), (), s32[]{:S(2)}) async-start(), calls=%async_computation.16 | async-start | bytes 3317760 | tf_op jit(solution)/shard_map/reduce_scatter | solution.py:266
  902.2 257.7 %reduce-scatter.14.cloned.1.call-start = ((), (), s32[]{:S(2)}) async-start(), calls=%async_computation.15 | async-start | bytes 9953280 | tf_op jit(solution)/shard_map/reduce_scatter | solution.py:263
  910.7 432.3 %reduce-scatter.18.cloned.1.call-start = ((), (), s32[]{:S(2)}) async-start(), calls=%async_computation.17 | async-start | bytes 13271040 | tf_op jit(solution)/shard_map/reduce_scatter | solution.py:269
  920.2 606.3 %reduce-scatter.20.cloned.1.call-start = ((), (), s32[]{:S(2)}) async-start(), calls=%async_computation.18 | async-start | bytes 13271040 | tf_op jit(solution)/shard_map/reduce_scatter | solution.py:272
  931.7 769.8 %all-reduce.14.cloned.1.call-start = ((), (), s32[]{:S(2)}) async-start(), calls=%async_computation.20 | async-start | bytes 23887872 | tf_op jit(solution)/shard_map/psum | solution.py:297
  1536.7 43.7 %copy-start.40 = (f32[1,1152]{1,0:T(1,128)S(1)}, f32[1,1152]{1,0:T(1,128)}, u32[]{:S(2)}) copy-start(f32[1,1152]{1,0:T(1,128)} %param.15) | copy-start | bytes 13828
  1536.8 43.7 %copy-start.42 = (f32[1,1152]{1,0:T(1,128)S(1)}, f32[1,1152]{1,0:T(1,128)}, u32[]{:S(2)}) copy-start(f32[1,1152]{1,0:T(1,128)} %copy-done.41) | copy-start | bytes 13828
  (49 other events, 164.0 us)
Sparse Core Ops, SparseCore 0:
  9.6 146.4 all-gather.8
  163.4 48.9 all-gather.12
  214.6 49.3 all-gather.10
  265.4 54.1 all-gather.14
  321.0 184.8 all-gather.16
  507.3 184.2 all-gather.18
  748.6 46.2 reduce-scatter.9
  797.7 47.5 reduce-scatter.11
  898.7 64.7 reduce-scatter.21
  966.2 52.8 reduce-scatter.15
  1022.1 137.7 reduce-scatter.13
  1162.2 180.6 reduce-scatter.17
  1345.3 181.1 reduce-scatter.19
  1532.2 169.2 all-reduce.13
where the time goes:
time: 1730 us; the launch traced here: 1720 us
  waiting for transfers between devices  1350 us (78%)
  matrix products  136 us (8%)
  blocking collectives  115 us (7%)
  other arithmetic  54.5 us (3%)
  local copies, waits for them, and re-layouts  47.8 us (3%)
  between operations  19.1 us (1%)
    reduce_scatter x1, waiting for transfers between devices, per_device(): lax.psum_scatter(local_grads[3].astype(jnp.bfloat16), 'narrow', scatter_d...  184 us
    reduce_scatter x1, waiting for transfers between devices, per_device(): lax.psum_scatter(local_grads[2].astype(jnp.bfloat16), 'narrow', scatter_d...  183 us
    all_gather x1, waiting for transfers between devices, per_device(): lax.all_gather(w_fc1, 'narrow', axis=0, tiled=True)  180 us
    all_gather x1, waiting for transfers between devices, per_device(): lax.all_gather(w_fc2, 'narrow', axis=0, tiled=True)  176 us
    reduce_scatter x1, waiting for transfers between devices, per_device(): lax.psum_scatter(local_grads[0].astype(jnp.bfloat16), 'narrow', scatter_d...  141 us
    psum x1, waiting for transfers between devices, per_device(): lax.psum(grad_wada.astype(jnp.bfloat16), 'wide').astype(jnp.float32)  120 us
    all_gather x1, waiting for transfers between devices, per_device(): lax.all_gather(w_qkv, 'narrow', axis=0, tiled=True)  93.1 us
    unnamed x3, blocking collectives  63.8 us
  transfers between devices with their start and end apart: 14, of which 14 were waited for; matrix products, arithmetic and copies ran while one was open for 7% of the time, Pallas kernels for 0%

commit v1 on v0

v1 whole, which is shorter than its diff:
```python
import jax
import jax.numpy as jnp
from jax import lax
from jax.sharding import PartitionSpec as P

HEADS = 16
F32 = jnp.float32
BF16 = jnp.bfloat16


def dot(left, right, dims=((1,), (0,))):
    return lax.dot_general(left, right, (dims, ((), ())), preferred_element_type=F32)


def ring(block, step):
    n = lax.axis_size("narrow")
    return lax.ppermute(block, "narrow", [(i, (i + step) % n) for i in range(n)])


def flip(block, bit):
    w = lax.axis_size("wide")
    return lax.ppermute(block, "wide", [(i, i ^ bit) for i in range(w)])


def hop(block, bit):
    return flip(block.astype(BF16), bit).astype(F32)


def ring_gather(block):
    n = lax.axis_size("narrow")
    return [block] + [ring(block, step) for step in range(1, n)]


def place(blocks, index_of, axis=0):
    buffer = jnp.zeros((len(blocks),) + blocks[0].shape, blocks[0].dtype)
    for j, block in enumerate(blocks):
        buffer = lax.dynamic_update_index_in_dim(buffer, block, index_of(j), 0)
    return buffer


def link_bits():
    w = lax.axis_size("wide")
    return [1 << k for k in range(1, w.bit_length()) if (1 << k) < w]


def plane_gather(block):
    links = link_bits()
    got = {0: block}
    if len(links) == 2:
        u, v = links
        half = block.shape[0] // 2
        got[u] = flip(block, u)
        got[v] = flip(block, v)
        got[u | v] = jnp.concatenate([flip(got[u][:half], v), flip(got[v][half:], u)], axis=0)
    else:
        for bit in links:
            for r in list(got):
                got[r | bit] = flip(got[r], bit)
    for r in list(got):
        got[r | 1] = flip(got[r], 1)
    return [got[r] for r in range(len(got))]


def plane_reduce(blocks):
    links = link_bits()
    even = {r: blocks[r] + hop(blocks[r | 1], 1) for r in range(0, len(blocks), 2)}
    if len(links) == 2:
        u, v = links
        half = blocks[0].shape[0] // 2
        corner = even[u | v]
        by_v = jnp.concatenate([even[v][:half] + hop(corner[:half], u), even[v][half:]], axis=0)
        by_u = jnp.concatenate([even[u][:half], even[u][half:] + hop(corner[half:], v)], axis=0)
        return even[0] + hop(by_u, u) + hop(by_v, v)
    for bit in reversed(links):
        for r in [r for r in even if r & bit]:
            even[r ^ bit] = even[r ^ bit] + hop(even.pop(r), bit)
    return even[0]


def quad_gather(block):
    p = lax.axis_index("wide")
    two = flip(block, 2)
    parts = [block, flip(block, 1), two, flip(two, 1)]
    return place(parts, lambda r: (p & 3) ^ r)


def quad_reduce(terms):
    w = lax.axis_size("wide")
    p = lax.axis_index("wide")
    part = [lax.dynamic_index_in_dim(terms, (p & 3) ^ r, 1, keepdims=False) for r in range(4)]
    total = part[0] + hop(part[1], 1) + hop(part[2] + hop(part[3], 1), 2)
    bit = 4
    while bit < w:
        low = total.astype(BF16)
        total = low.astype(F32) + flip(low, bit).astype(F32)
        bit *= 2
    return total.astype(BF16)


def rows_mean(rows_in):
    return jnp.mean(rows_in, axis=-1, keepdims=True)


def norm_parts(rows_in):
    centered = rows_in - rows_mean(rows_in)
    inv = lax.rsqrt(rows_mean(centered * centered) + 1e-06)
    return centered * inv, inv


def norm_back(unit, inv, grad_unit):
    return inv * (grad_unit - rows_mean(grad_unit) - unit * rows_mean(grad_unit * unit))


def per_device(
    x_input,
    condition,
    counts,
    w_ada,
    b_ada,
    w_qkv,
    qv_bias,
    w_out,
    b_out,
    w_fc1,
    b_fc1,
    w_fc2,
    b_fc2,
    d_out,
):
    n = lax.axis_size("narrow")
    w = lax.axis_size("wide")
    z = lax.axis_index("narrow")
    p = lax.axis_index("wide")
    slot_count, tokens, width = x_input.shape
    x_rows = x_input.reshape(tokens, width)
    heads = HEADS // n
    head_size = width // HEADS
    score_scale = head_size ** (-0.5)
    shard = width // n
    sub = shard // 4
    hidden_dev = w_fc2.shape[0] // w
    hidden_all = n * hidden_dev
    cols = heads * head_size

    def ahead(j):
        return lax.rem(z + j, n)

    def behind(j):
        return lax.rem(z + n - j, n)

    living = (counts[0] > 0).astype(F32)

    cond_act, silu_pull = jax.vjp(jax.nn.silu, condition)
    cond_low = cond_act.astype(BF16)
    mod_part = dot(cond_low, w_ada)[0] + b_ada.astype(F32)
    unit_one, inv_one = norm_parts(x_rows)
    unit_low = unit_one.astype(BF16)
    small = jnp.concatenate([mod_part] + [v.astype(F32) for v in (qv_bias, b_out, b_fc1, b_fc2)])
    small_all = place(ring_gather(small), behind)
    ends = [0]
    for piece in (mod_part, qv_bias, b_out, b_fc1, b_fc2):
        ends.append(ends[-1] + piece.shape[0])
    modulation, qv_full, bout_full, bfc1_full, bfc2_full = [
        small_all[:, low:high].reshape(-1) for low, high in zip(ends[:-1], ends[1:])
    ]
    shift_one, scale_one, gate_one, shift_two, scale_two, gate_two = [
        modulation[None, k * width : (k + 1) * width] for k in range(6)
    ]

    unit_blocks = ring_gather(unit_low)

    qkv_mine = lax.dynamic_slice_in_dim(w_qkv, (p & 3) * sub, sub, 0)
    qkv_to = qkv_mine.reshape(sub, 3, n, cols).transpose(2, 0, 1, 3).reshape(n, sub, 3 * cols)
    qkv_got = [
        ring(lax.dynamic_index_in_dim(qkv_to, ahead(j), 0, keepdims=False), j) if j else
        lax.dynamic_index_in_dim(qkv_to, z, 0, keepdims=False)
        for j in range(n)
    ]
    qkv_cols = quad_gather(place(qkv_got, behind)).transpose(1, 0, 2, 3).reshape(width, 3 * cols)

    out_mine = lax.dynamic_slice_in_dim(w_out, (p & 3) * sub, sub, 0)
    out_blocks = ring_gather(out_mine)
    out_stack = jnp.stack([out_blocks[(n - j) % n] for j in range(n)])
    out_cat = quad_gather(out_stack).transpose(1, 0, 2, 3).reshape(width, width)

    fc1_mine = lax.dynamic_index_in_dim(
        w_fc1.reshape(shard, n, w, hidden_dev), p, 2, keepdims=False
    ).reshape(shard, hidden_all)
    fc1_dev = place(ring_gather(fc1_mine), behind).reshape(width, hidden_all)
    fc2_mine = lax.dynamic_slice_in_dim(w_fc2, p * hidden_dev, hidden_dev, 0)
    fc2_dev = place(ring_gather(fc2_mine), behind).reshape(hidden_all, width)
    bfc1_dev = lax.dynamic_index_in_dim(bfc1_full.reshape(n, w, hidden_dev), p, 1, keepdims=False)
    bfc1_dev = bfc1_dev.reshape(1, hidden_all)

    first_all = jnp.concatenate(
        [(b.astype(F32) * (1.0 + scale_one) + shift_one).astype(BF16) for b in unit_blocks], axis=0
    )
    qv_two = qv_full.reshape(2, n, cols)
    q_bias = lax.dynamic_index_in_dim(qv_two[0], z, 0, keepdims=True)
    v_bias = lax.dynamic_index_in_dim(qv_two[1], z, 0, keepdims=True)
    bias_three = jnp.concatenate([q_bias, jnp.zeros_like(q_bias), v_bias], axis=1)
    projected = (dot(first_all, qkv_cols) + bias_three).astype(BF16)
    image = n * tokens
    queries = projected[:, :cols].reshape(image, heads, head_size)
    keys = projected[:, cols : 2 * cols].reshape(image, heads, head_size)
    values = projected[:, 2 * cols :].reshape(image, heads, head_size)
    scores = jnp.einsum("qhd,khd->hqk", queries, keys, preferred_element_type=F32) * score_scale
    row_max = jnp.max(scores, axis=-1, keepdims=True)
    exponent = jnp.exp(scores - row_max)
    row_total = jnp.sum(exponent, axis=-1, keepdims=True)
    lse = row_max + jnp.log(row_total)
    attention = (exponent / row_total).astype(BF16)
    mixed = jnp.einsum("hqk,khd->qhd", attention, values, preferred_element_type=F32)
    mixed = mixed.astype(BF16).reshape(n, tokens, cols)
    mixed_cat = jnp.concatenate(
        [mixed[0]] + [ring(mixed[j], n - j) for j in range(1, n)], axis=1
    )

    branch_one = dot(mixed_cat, out_cat) + bout_full[None]
    middle = x_rows + gate_one * branch_one
    unit_two, inv_two = norm_parts(middle)
    second_low = (unit_two * (1.0 + scale_two) + shift_two).astype(BF16)

    grad_out = living * d_out.reshape(tokens, width)
    grad_two = (gate_two * grad_out).astype(BF16)
    two_all = jnp.concatenate(plane_gather(grad_two), axis=0)
    second_all = jnp.concatenate(plane_gather(second_low), axis=0)
    hidden_pre = dot(second_all, fc1_dev) + bfc1_dev
    active_pre, gelu_pull = jax.vjp(lambda v: jax.nn.gelu(v, approximate=True), hidden_pre)
    active = active_pre.astype(BF16)
    grad_active = dot(two_all, fc2_dev, ((1,), (1,)))
    grad_hidden = gelu_pull(grad_active)[0].astype(BF16)
    second_terms = dot(grad_hidden, fc1_dev, ((1,), (1,))).reshape(w, tokens, width)
    grad_second = plane_reduce([second_terms[r] for r in range(w)])
    two_terms = dot(active, fc2_dev).reshape(w, tokens, width)
    branch_two = plane_reduce([two_terms[r] for r in range(w)]) + bfc2_full[None]
    result = living * (middle + gate_two * branch_two)
    grad_gate_two = jnp.sum(grad_out * branch_two, axis=0)

    def narrow_sum(terms):
        low = terms.astype(BF16)
        got = [lax.dynamic_index_in_dim(low, z, 0, keepdims=False)]
        got += [
            ring(lax.dynamic_index_in_dim(low, ahead(j), 0, keepdims=False), j) for j in range(1, n)
        ]
        return sum(g.astype(F32) for g in got)

    wfc2_own = narrow_sum(dot(active, two_all, ((0,), (0,))).reshape(n, hidden_dev, width))
    grad_wfc2 = place(plane_gather(wfc2_own.astype(BF16)), lambda r: p ^ r)
    grad_wfc2 = grad_wfc2.reshape(w * hidden_dev, width).astype(F32)
    wfc1_own = narrow_sum(dot(second_all, grad_hidden, ((0,), (0,))).reshape(n, shard, hidden_all))
    grad_wfc1 = place(plane_gather(wfc1_own.astype(BF16)), lambda r: p ^ r)
    grad_wfc1 = grad_wfc1.reshape(w, shard, n, hidden_dev).transpose(1, 2, 0, 3)
    grad_wfc1 = grad_wfc1.reshape(shard, n * w * hidden_dev).astype(F32)
    bfc1_terms = jnp.sum(grad_hidden.astype(F32), axis=0)
    bfc2_terms = jnp.sum(grad_two.astype(F32), axis=0)

    grad_shift_two = jnp.sum(grad_second, axis=0)
    grad_scale_two = jnp.sum(grad_second * unit_two, axis=0)
    grad_middle = grad_out + norm_back(unit_two, inv_two, grad_second * (1.0 + scale_two))
    grad_one = (gate_one * grad_middle).astype(BF16)
    grad_gate_one = jnp.sum(grad_middle * branch_one, axis=0)
    bout_terms = jnp.sum(grad_one.astype(F32), axis=0)
    grad_mixed_cat = dot(grad_one, out_cat, ((1,), (1,))).astype(BF16).reshape(tokens, n, cols)
    grad_mixed = jnp.concatenate(
        [grad_mixed_cat[:, 0]] + [ring(grad_mixed_cat[:, j], j) for j in range(1, n)], axis=0
    ).reshape(image, heads, head_size)
    wout_terms = dot(mixed_cat, grad_one, ((0,), (0,))).reshape(n, 4, sub, width)
    wout_quad = quad_reduce(wout_terms)
    wout_own = wout_quad[0].astype(F32) + sum(
        ring(wout_quad[j], j).astype(F32) for j in range(1, n)
    )
    grad_wout = quad_gather(wout_own.astype(BF16)).reshape(shard, width).astype(F32)

    scores = jnp.einsum("qhd,khd->hqk", queries, keys, preferred_element_type=F32) * score_scale
    weights = jnp.exp(scores - lse)
    grad_attention = jnp.einsum("qhd,khd->hqk", grad_mixed, values, preferred_element_type=F32)
    delta = jnp.sum(weights * grad_attention, axis=-1, keepdims=True)
    grad_scores = (weights * (grad_attention - delta)).astype(BF16)
    grad_queries = (
        jnp.einsum("hqk,khd->qhd", grad_scores, keys, preferred_element_type=F32) * score_scale
    )
    grad_keys = (
        jnp.einsum("hqk,qhd->khd", grad_scores, queries, preferred_element_type=F32) * score_scale
    )
    grad_values = jnp.einsum(
        "hqk,qhd->khd", weights.astype(BF16), grad_mixed, preferred_element_type=F32
    )
    grad_projected = jnp.concatenate(
        [g.astype(BF16).reshape(image, cols) for g in (grad_queries, grad_keys, grad_values)], axis=1
    )
    first_terms = dot(grad_projected, qkv_cols, ((1,), (1,)))
    unit_all = jnp.concatenate(unit_blocks, axis=0)
    grad_shift_one = jnp.sum(first_terms, axis=0)
    grad_scale_one = jnp.sum(first_terms * unit_all.astype(F32), axis=0)
    first_low = first_terms.astype(BF16).reshape(n, tokens, width)
    grad_first = first_low[0].astype(F32) + sum(
        ring(first_low[j], n - j).astype(F32) for j in range(1, n)
    )
    grad_input = grad_middle + norm_back(unit_one, inv_one, grad_first * (1.0 + scale_one))

    wqkv_terms = dot(first_all, grad_projected, ((0,), (0,))).reshape(n, 4, sub, 3 * cols)
    wqkv_quad = quad_reduce(wqkv_terms)
    wqkv_got = [lax.dynamic_index_in_dim(wqkv_quad, z, 0, keepdims=False)] + [
        ring(lax.dynamic_index_in_dim(wqkv_quad, ahead(j), 0, keepdims=False), j)
        for j in range(1, n)
    ]
    wqkv_all = quad_gather(place(wqkv_got, behind))
    grad_wqkv = wqkv_all.reshape(4, n, sub, 3, cols).transpose(0, 2, 3, 1, 4)
    grad_wqkv = grad_wqkv.reshape(shard, 3 * width).astype(F32)
    projected_sums = jnp.sum(grad_projected.astype(F32), axis=0).reshape(3, cols)

    mod_terms = jnp.concatenate(
        [grad_shift_one, grad_scale_one, grad_gate_one, grad_shift_two, grad_scale_two, grad_gate_two]
    ).reshape(n, -1)
    qv_terms = jnp.zeros((2, n, cols), F32)
    qv_terms = lax.dynamic_update_slice(
        qv_terms, jnp.stack([projected_sums[0], projected_sums[2]])[:, None], (0, z, 0)
    )
    bfc1_wide = lax.dynamic_update_slice(
        jnp.zeros((n, w, hidden_dev), F32), bfc1_terms.reshape(n, 1, hidden_dev), (0, p, 0)
    )
    small_terms = jnp.concatenate(
        [
            mod_terms,
            qv_terms.reshape(n, -1),
            bout_terms.reshape(n, -1),
            bfc1_wide.reshape(n, -1),
            bfc2_terms.reshape(n, -1),
        ],
        axis=1,
    )
    small_own = lax.dynamic_index_in_dim(small_terms, z, 0, keepdims=False) + sum(
        ring(lax.dynamic_index_in_dim(small_terms, ahead(j), 0, keepdims=False), j)
        for j in range(1, n)
    )
    mod_size = mod_terms.shape[1]
    mod_low = small_own[:mod_size].astype(BF16)
    cond_part = dot(mod_low[None], w_ada, ((1,), (1,)))
    cond_total = cond_part + sum(ring(cond_part, j) for j in range(1, n))
    grad_condition = silu_pull(cond_total)[0]
    shared = jnp.concatenate([small_own, cond_act[0]])[None]
    bits = [1] + link_bits()
    for bit in bits:
        shared = jnp.concatenate([shared, flip(shared, bit)], axis=0)
    order = jnp.arange(w) ^ p
    shared = shared[order]
    mod_rows = shared[:, :mod_size].astype(BF16)
    cond_rows = shared[:, small_own.shape[0] :].astype(BF16)
    grad_wada = dot(cond_rows, mod_rows, ((0,), (0,)))
    grad_bada = jnp.sum(mod_rows.astype(F32), axis=0)
    bias_sums = jnp.sum(shared[:, mod_size : small_own.shape[0]], axis=0)
    ends = [0]
    for piece in (qv_bias, b_out, b_fc1, b_fc2):
        ends.append(ends[-1] + piece.shape[0])
    grad_qv, grad_bout, grad_bfc1, grad_bfc2 = [
        bias_sums[low:high] for low, high in zip(ends[:-1], ends[1:])
    ]
    return (
        result[None],
        grad_input[None],
        grad_condition,
        grad_wada,
        grad_bada,
        grad_wqkv,
        grad_qv,
        grad_wout,
        grad_bout,
        grad_wfc1,
        grad_bfc1,
        grad_wfc2,
        grad_bfc2,
    )


def solution(mesh):
    in_specs = (
        P("wide", "narrow", None),
        P("wide", None),
        P("wide"),
        P(None, "narrow"),
        P("narrow"),
        P("narrow", None),
        P("narrow"),
        P("narrow", None),
        P("narrow"),
        P("narrow", None),
        P("narrow"),
        P("narrow", None),
        P("narrow"),
        P("wide", "narrow", None),
    )
    out_specs = (
        P("wide", "narrow", None),
        P("wide", "narrow", None),
        P("wide", None),
        P(None, "narrow"),
        P("narrow"),
        P("narrow", None),
        P("narrow"),
        P("narrow", None),
        P("narrow"),
        P("narrow", None),
        P("narrow"),
        P("narrow", None),
        P("narrow"),
    )
    return jax.shard_map(
        per_device, mesh=mesh, in_specs=in_specs, out_specs=out_specs, check_vma=False
    )
```

time: 1730 us -> 738 us (0.43)
  waiting for transfers between devices: 1350 us -> 233 us
  starting transfers between devices: 0.97 us -> 150 us
  local copies, waits for them, and re-layouts: 47.8 us -> 165 us
  blocking collectives: 115 us -> 0 us
  matrix products: 136 us -> 108 us
    reduce_scatter x6 -> x0, waiting for transfers between devices: 634 us -> none  [the longest x1 184 us: per_device(): lax.psum_scatter(local_grads[3].astype(jnp.bfloat16), 'narrow', scatter_d...]
    all_gather x6 -> x0, waiting for transfers between devices: 562 us -> none  [the longest x1 180 us: per_device(): lax.all_gather(w_fc1, 'narrow', axis=0, tiled=True)]
    ppermute x0 -> x116, waiting for transfers between devices: none -> 233 us  [the longest x45 143 us: ring(): lax.ppermute(block, 'narrow', [(i, (i + step) % n) for i in range(n)])]
    ppermute x0 -> x116, starting transfers between devices: none -> 150 us  [the longest x45 104 us: ring(): lax.ppermute(block, 'narrow', [(i, (i + step) % n) for i in range(n)])]
    psum x1 -> x0, waiting for transfers between devices: 120 us -> none  [per_device(): lax.psum(grad_wada.astype(jnp.bfloat16), 'wide').astype(jnp.float32)]
    unnamed x3 -> x0, blocking collectives: 63.8 us -> none
    dynamic_update_slice x0 -> x49, local copies, waits for them, and re-layouts: none -> 42.4 us  [the longest x47 42.3 us: place(): buffer = lax.dynamic_update_index_in_dim(buffer, block, index_of(j), 0)]
    psum x2 -> x0, blocking collectives: 37.7 us -> none  [the longest x1 25.9 us: per_device(): lax.psum(grad_bada.astype(jnp.bfloat16), 'wide').astype(jnp.float32)]
  transfers between devices with their start and end apart: 14 -> 116, of which waited for: 14 -> 41; matrix products, arithmetic and copies ran while one was open for 7% -> 31% of each run, Pallas kernels for 0% -> 0%
where the time goes in v1:
time: 738 us; the launch traced here: 729 us
  waiting for transfers between devices  233 us (32%)
  local copies, waits for them, and re-layouts  165 us (22%)
  starting transfers between devices  150 us (20%)
  matrix products  108 us (15%)
  other arithmetic  69.2 us (9%)
    ppermute x45, waiting for transfers between devices, ring(): lax.ppermute(block, 'narrow', [(i, (i + step) % n) for i in range(n)])  143 us
    ppermute x45, starting transfers between devices, ring(): lax.ppermute(block, 'narrow', [(i, (i + step) % n) for i in range(n)])  104 us
    ppermute x71, waiting for transfers between devices, flip(): return lax.ppermute(block, 'wide', [(i, i ^ bit) for i in range(w)])  89.5 us
    dot_general x15, matrix products, dot(): lax.dot_general(left, right, (dims, ((), ())), preferred_element_type=F32)  64.7 us
    ppermute x71, starting transfers between devices, flip(): return lax.ppermute(block, 'wide', [(i, i ^ bit) for i in range(w)])  45.9 us
    dynamic_update_slice x47, local copies, waits for them, and re-layouts, place(): buffer = lax.dynamic_update_index_in_dim(buffer, block, index_of(j), 0)  42.3 us
    unnamed x220, local copies, waits for them, and re-layouts  23.9 us
    convert_element_type x3, local copies, waits for them, and re-layouts, per_device(): grad_wqkv = grad_wqkv.reshape(shard, 3 * width).astype(F32)  23.9 us
  transfers between devices with their start and end apart: 116, of which 41 were waited for; matrix products, arithmetic and copies ran while one was open for 31% of the time, Pallas kernels for 0%

profile of v1, /device:TPU:0, one launch (start us, length us, event | category | flops | bytes accessed | tf_op | source)
XLA Modules:
  0.0 729.0 jit_solution(16979784872620804687)
XLA Ops:
  51.4 8.9 %collective-permute-done.8 = bf16[72,864]{1,0:T(8,128)(2,1)S(1)} collective-permute-done((bf16[72,864]{1,0:T(8,128)(2,1)S(1)}, bf16[72,864]{1,0:T(8,128)(2,1)S(1)}, u32[]{:S(2)}, u32[]{:S(2)}) %collective-permute-start.8) | collective-permute-done | bytes 124448 | tf_op jit(solution)/shard_map/ppermute | solution.py:17
  75.2 8.6 %collective-permute-done.30 = bf16[288,576]{0,1:T(8,128)(2,1)} collective-permute-done((bf16[288,576]{0,1:T(8,128)(2,1)S(1)}, bf16[288,576]{0,1:T(8,128)(2,1)}, u32[]{:S(2)}, u32[]{:S(2)}) %collective-permute-start.30) | collective-permute-done | bytes 331808 | tf_op jit(solution)/shard_map/ppermute | solution.py:17
  83.8 21.3 %collective-permute-start.3 = (bf16[256,1152]{1,0:T(8,128)(2,1)}, bf16[256,1152]{1,0:T(8,128)(2,1)}, u32[]{:S(2)}, u32[]{:S(2)}) collective-permute-start(bf16[256,1152]{1,0:T(8,128)(2,1)} %get-tuple-element.67), channel_id=1, source_target_pairs={{0,1},{1,2},{2,3},{3,0},{4,5},{5,6},{6,7},{7,4},{8,9},{9,10},{10,1... | collective-permute-start | bytes 1769480 | tf_op jit(solution)/shard_map/ppermute | solution.py:17
  107.0 9.3 %collective-permute-start.4 = (bf16[256,1152]{1,0:T(8,128)(2,1)}, bf16[256,1152]{1,0:T(8,128)(2,1)}, u32[]{:S(2)}, u32[]{:S(2)}) collective-permute-start(bf16[256,1152]{1,0:T(8,128)(2,1)} %get-tuple-element.67), channel_id=1, source_target_pairs={{0,2},{1,3},{2,0},{3,1},{4,6},{5,7},{6,4},{7,5},{8,10},{9,11},{10,... | collective-permute-start | bytes 1769480 | tf_op jit(solution)/shard_map/ppermute | solution.py:17
  125.7 11.2 %collective-permute-done.33 = bf16[144,1152]{1,0:T(8,128)(2,1)} collective-permute-done((bf16[144,1152]{1,0:T(8,128)(2,1)}, bf16[144,1152]{1,0:T(8,128)(2,1)}, u32[]{:S(2)}, u32[]{:S(2)}) %collective-permute-start.33) | collective-permute-done | bytes 331808 | tf_op jit(solution)/shard_map/ppermute | solution.py:17
  144.1 7.6 %collective-permute-done.44 = bf16[256,1152]{1,0:T(8,128)(2,1)S(1)} collective-permute-done((bf16[256,1152]{1,0:T(8,128)(2,1)S(1)}, bf16[256,1152]{1,0:T(8,128)(2,1)S(1)}, u32[]{:S(2)}, u32[]{:S(2)}) %collective-permute-start.44) | collective-permute-done | bytes 589856 | tf_op jit(solution)/shard_map/ppermute | solution.py:22
  171.8 12.0 %collective-permute-done.19 = bf16[4,72,1152]{2,1,0:T(8,128)(2,1)S(1)} collective-permute-done((bf16[4,72,1152]{2,1,0:T(8,128)(2,1)S(1)}, bf16[4,72,1152]{2,1,0:T(8,128)(2,1)S(1)}, u32[]{:S(2)}, u32[]{:S(2)}) %collective-permute-start.19) | collective-permute-done | bytes 663584 | tf_op jit(solution)/shard_map/ppermute | solution.py:22
  195.9 8.1 %multiply_reduce_fusion.1 = (f32[4,1024]{1,0:T(4,128)S(1)}, f32[4,1024,1024]{1,2,0:T(8,128)}) fusion(bf16[1024,4,72]{0,2,1:T(8,128)(2,1)S(1)} %bitcast.300, bf16[1024,4,72]{0,2,1:T(8,128)(2,1)S(1)} %bitcast.302), kind=kOutput, calls=%fused_computation.7 | convolution fusion | flops 612364288 | bytes 17973248 | tf_op jit(solution)/shard_map/qhd,khd->hqk/dot_general | solution.py:207
  204.1 8.5 %fusion = f32[4,1024]{1,0:T(4,128)S(1)} fusion(f32[4,1024,1024]{1,2,0:T(8,128)} %get-tuple-element.153, f32[4,1024]{1,0:T(4,128)S(1)} %get-tuple-element.152), kind=kLoop, calls=%fused_computation.6 | loop fusion | flops 12578816 | bytes 16809984 | tf_op jit(solution)/shard_map/reduce_sum | solution.py:210
  212.6 7.9 %fusion.21 = bf16[1024,4,72]{0,2,1:T(8,128)(2,1)S(1)} fusion(bf16[1024,4,72]{0,2,1:T(8,128)(2,1)S(1)} %bitcast.307, f32[4,1024,1024]{1,2,0:T(8,128)} %get-tuple-element.153, f32[4,1024]{1,0:T(4,128)S(1)} %fusion, f32[4,1024]{1,0:T(4,128)S(1)} %get-tuple-element.152), kind=kOutput, calls=%fused_computation.47 | convolution fusion | flops 621051904 | bytes 17989632 | tf_op jit(solution)/shard_map/hqk,khd->qhd/dot_general | solution.py:213
  220.5 5.9 collective-permute-start.12
  232.7 7.5 %collective-permute-done.13 = bf16[256,288]{0,1:T(8,128)(2,1)S(1)} collective-permute-done((bf16[256,288]{0,1:T(8,128)(2,1)S(1)}, bf16[256,288]{0,1:T(8,128)(2,1)S(1)}, u32[]{:S(2)}, u32[]{:S(2)}) %collective-permute-start.13) | collective-permute-done | bytes 147488 | tf_op jit(solution)/shard_map/ppermute | solution.py:17
  249.5 10.5 %collective-permute-done.22 = bf16[256,1152]{1,0:T(8,128)(2,1)S(1)} collective-permute-done((bf16[256,1152]{1,0:T(8,128)(2,1)S(1)}, bf16[256,1152]{1,0:T(8,128)(2,1)S(1)}, u32[]{:S(2)}, u32[]{:S(2)}) %collective-permute-start.22) | collective-permute-done | bytes 589856 | tf_op jit(solution)/shard_map/ppermute | solution.py:22
  279.1 6.3 convert_reduce_fusion
  289.7 7.3 %fusion.97 = (bf16[2048,1152]{1,0:T(8,128)(2,1)}, f32[2048,1152]{1,0:T(8,128)}) fusion(bf16[2048,576]{0,1:T(8,128)(2,1)S(1)} %get-tuple-element.54, bf16[1152,576]{1,0:T(8,128)(2,1)S(1)} %bitcast.330), kind=kOutput, calls=%fused_computation.309 | convolution fusion | flops 2720268288 | bytes 17842176 | tf_op jit(solution)/shard_map/dot_general | solution.py:12
  297.0 7.9 %fusion.96 = (bf16[2048,1152]{1,0:T(8,128)(2,1)}, f32[2048,1152]{1,0:T(8,128)}) fusion(bf16[576,1152]{1,0:T(8,128)(2,1)S(1)} %bitcast.337, f32[2048,576]{0,1:T(8,128)S(1)} %fusion.98, f32[576]{0:T(1024)S(1)} %copy-done.87), kind=kOutput, calls=%fused_computation.308 | convolution fusion | flops 2732064768 | bytes 20203776 | tf_op jit(solution)/shard_map/dot_general | solution.py:12
  321.9 11.9 %collective-permute-done.94 = bf16[288,576]{1,0:T(8,128)(2,1)} collective-permute-done((bf16[288,576]{1,0:T(8,128)(2,1)}, bf16[288,576]{1,0:T(8,128)(2,1)}, u32[]{:S(2)}, u32[]{:S(2)}) %collective-permute-start.94) | collective-permute-done | bytes 331808 | tf_op jit(solution)/shard_map/ppermute | solution.py:17
  334.0 21.7 %collective-permute-done.95 = bf16[288,576]{1,0:T(8,128)(2,1)} collective-permute-done((bf16[288,576]{1,0:T(8,128)(2,1)}, bf16[288,576]{1,0:T(8,128)(2,1)}, u32[]{:S(2)}, u32[]{:S(2)}) %collective-permute-start.95) | collective-permute-done | bytes 331808 | tf_op jit(solution)/shard_map/ppermute | solution.py:17
  363.2 5.5 collective-permute-done.107
  462.1 6.6 copy.94
  472.0 11.7 %collective-permute-done.42 = bf16[256,1152]{1,0:T(8,128)(2,1)S(1)} collective-permute-done((bf16[256,1152]{1,0:T(8,128)(2,1)S(1)}, bf16[256,1152]{1,0:T(8,128)(2,1)S(1)}, u32[]{:S(2)}, u32[]{:S(2)}) %collective-permute-start.42) | collective-permute-done | bytes 589856 | tf_op jit(solution)/shard_map/ppermute | solution.py:22
  490.8 7.6 %collective-permute-start.59 = (bf16[256,288]{0,1:T(8,128)(2,1)S(1)}, bf16[256,288]{0,1:T(8,128)(2,1)S(1)}, u32[]{:S(2)}, u32[]{:S(2)}) collective-permute-start(bf16[256,288]{0,1:T(8,128)(2,1)S(1)} %get-tuple-element.112), channel_id=1, source_target_pairs={{0,1},{1,2},{2,3},{3,0},{4,5},{5,6},{6,7},{7,4},{8,9},{9,10},{10,1... | collective-permute-start | bytes 442376 | tf_op jit(solution)/shard_map/ppermute | solution.py:17
  510.5 15.3 %multiply_reduce_fusion = (f32[4,1024]{1,0:T(4,128)S(1)}, f32[4,1024,1024]{1,2,0:T(8,128)}) fusion(f32[4,1024,1024]{1,2,0:T(8,128)} %get-tuple-element.153, f32[4,1024]{1,0:T(4,128)S(1)} %log_add_fusion, bf16[1024,4,72]{0,2,1:T(8,128)(2,1)S(1)} %bitcast.308, bf16[256,4,72]{0,2,1:T(8,128)(2,1)S(1)} %bitcast.346, bf16[256,4,72]{0,2,1:T(8,128)(2,1)S(1)} %bitcast.344, ...), kind=kOutput, calls=%fused_computation.2 | convolution fusion | flops 623112192 | bytes 34766848 | tf_op jit(solution)/shard_map/qhd,khd->hqk/dot_general | solution.py:277
  526.1 8.2 %multiply_convert_fusion = bf16[4,1024,1024]{1,2,0:T(8,128)(2,1)S(1)} fusion(f32[4,1024,1024]{1,2,0:T(8,128)} %get-tuple-element.160, f32[4,1024,1024]{1,2,0:T(8,128)S(1)} %bitcast.294, f32[4,1024]{1,0:T(4,128)S(1)} %get-tuple-element.159, f32[4,1024]{1,0:T(4,128)S(1)} %log_add_fusion), kind=kLoop, calls=%fused_computation.1 | loop fusion | flops 20971520 | bytes 41975808 | tf_op jit(solution)/shard_map/convert_element_type | solution.py:279
  538.6 7.7 %fusion.17 = bf16[4,72,1024]{2,1,0:T(8,128)(2,1)S(1)} fusion(f32[4,1024,1024]{1,2,0:T(8,128)} %get-tuple-element.153, f32[4,1024]{1,0:T(4,128)S(1)} %log_add_fusion, bf16[256,4,72]{0,2,1:T(8,128)(2,1)S(1)} %bitcast.347, bf16[256,4,72]{0,2,1:T(8,128)(2,1)S(1)} %bitcast.345, bf16[256,4,72]{0,2,1:T(8,128)(2,1)S(1)} %bitcast.343, ...), kind=kOutput, calls=%fused_computation.45 | convolution fusion | flops 619216896 | bytes 17973248 | tf_op jit(solution)/shard_map/hqk,qhd->khd/dot_general | solution.py:286
  546.4 5.3 multiply_reduce_fusion.2
  558.8 11.8 %collective-permute-done.62 = bf16[256,1152]{1,0:T(8,128)(2,1)} collective-permute-done((bf16[256,1152]{1,0:T(8,128)(2,1)}, bf16[256,1152]{1,0:T(8,128)(2,1)}, u32[]{:S(2)}, u32[]{:S(2)}) %collective-permute-start.62) | collective-permute-done | bytes 589856 | tf_op jit(solution)/shard_map/ppermute | solution.py:17
  570.6 39.1 %collective-permute-done.63 = bf16[256,1152]{1,0:T(8,128)(2,1)} collective-permute-done((bf16[256,1152]{1,0:T(8,128)(2,1)}, bf16[256,1152]{1,0:T(8,128)(2,1)}, u32[]{:S(2)}, u32[]{:S(2)}) %collective-permute-start.63) | collective-permute-done | bytes 589856 | tf_op jit(solution)/shard_map/ppermute | solution.py:17
  643.7 6.3 collective-permute-done.76
  704.9 8.8 %reshape.329 = f32[4,4,72,3,288]{4,3,2,1,0:T(4,128)} reshape(bf16[4,4,72,864]{3,2,1,0:T(8,128)(2,1)} %bitcast_dynamic-update-slice_fusion.4) | data formatting | bytes 5971968 | tf_op jit(solution)/shard_map/convert_element_type | solution.py:310
  713.7 9.0 %copy.82 = f32[4,72,3,4,288]{4,3,2,1,0:T(4,128)} copy(f32[4,72,3,4,288]{4,2,1,3,0:T(4,128)} %bitcast.299) | data formatting | bytes 7962624 | tf_op jit(solution)/shard_map/convert_element_type | solution.py:310
  722.7 6.1 reshape.322
  (663 shorter events, 393.8 us)
Async XLA Ops:
  4.3 27.2 %collective-permute-start = (f32[4032]{0:T(1024)S(1)}, f32[4032]{0:T(1024)}, u32[]{:S(2)}, u32[]{:S(2)}) collective-permute-start(f32[4032]{0:T(1024)S(1)} %concatenate.86), channel_id=1, source_target_pairs={{0,1},{1,2},{2,3},{3,0},{4,5},{5,6},{6,7},{7,4},{8,9},{9,10},{10,1... | collective-permute-start | bytes 48392 | tf_op jit(solution)/shard_map/ppermute | solution.py:17
  7.4 25.2 %collective-permute-start.1 = (f32[4032]{0:T(1024)S(1)}, f32[4032]{0:T(1024)}, u32[]{:S(2)}, u32[]{:S(2)}) collective-permute-start(f32[4032]{0:T(1024)S(1)} %concatenate.86), channel_id=1, source_target_pairs={{0,2},{1,3},{2,0},{3,1},{4,6},{5,7},{6,4},{7,5},{8,10},{9,11},{10,... | collective-permute-start | bytes 48392 | tf_op jit(solution)/shard_map/ppermute | solution.py:17
  10.0 25.3 %collective-permute-start.2 = (f32[4032]{0:T(1024)S(1)}, f32[4032]{0:T(1024)S(1)}, u32[]{:S(2)}, u32[]{:S(2)}) collective-permute-start(f32[4032]{0:T(1024)S(1)} %concatenate.86), channel_id=1, source_target_pairs={{0,3},{1,0},{2,1},{3,2},{4,7},{5,4},{6,5},{7,6},{8,11},{9,8},{10,9... | collective-permute-start | bytes 48392 | tf_op jit(solution)/shard_map/ppermute | solution.py:17
  12.0 50.6 %collective-permute-start.15 = (bf16[72,1152]{1,0:T(8,128)(2,1)}, bf16[72,1152]{1,0:T(8,128)(2,1)S(1)}, u32[]{:S(2)}, u32[]{:S(2)}) collective-permute-start(bf16[72,1152]{1,0:T(8,128)(2,1)} %constant_dynamic-slice_fusion.7), channel_id=1, source_target_pairs={{0,3},{1,0},{2,1},{3,2},{4,7},{5,4},{6,5},{7,6},{8,11},{9,8},{10,9... | collective-permute-start | bytes 497672 | tf_op jit(solution)/shard_map/ppermute | solution.py:17
  12.4 51.6 %collective-permute-start.16 = (bf16[72,1152]{1,0:T(8,128)(2,1)}, bf16[72,1152]{1,0:T(8,128)(2,1)}, u32[]{:S(2)}, u32[]{:S(2)}) collective-permute-start(bf16[72,1152]{1,0:T(8,128)(2,1)} %constant_dynamic-slice_fusion.7), channel_id=1, source_target_pairs={{0,2},{1,3},{2,0},{3,1},{4,6},{5,7},{6,4},{7,5},{8,10},{9,11},{10,... | collective-permute-start | bytes 497672 | tf_op jit(solution)/shard_map/ppermute | solution.py:17
  31.6 33.1 %collective-permute-start.17 = (bf16[72,1152]{1,0:T(8,128)(2,1)}, bf16[72,1152]{1,0:T(8,128)(2,1)S(1)}, u32[]{:S(2)}, u32[]{:S(2)}) collective-permute-start(bf16[72,1152]{1,0:T(8,128)(2,1)} %constant_dynamic-slice_fusion.7), channel_id=1, source_target_pairs={{0,1},{1,2},{2,3},{3,0},{4,5},{5,6},{6,7},{7,4},{8,9},{9,10},{10,1... | collective-permute-start | bytes 497672 | tf_op jit(solution)/shard_map/ppermute | solution.py:17
  62.6 44.5 %collective-permute-start.31 = (bf16[288,576]{0,1:T(8,128)(2,1)S(1)}, bf16[288,576]{0,1:T(8,128)(2,1)}, u32[]{:S(2)}, u32[]{:S(2)}) collective-permute-start(bf16[288,576]{0,1:T(8,128)(2,1)S(1)} %bitcast.328), channel_id=1, source_target_pairs={{0,3},{1,0},{2,1},{3,2},{4,7},{5,4},{6,5},{7,6},{8,11},{9,8},{10,9... | collective-permute-start | bytes 995336 | tf_op jit(solution)/shard_map/ppermute | solution.py:17
  64.0 56.2 %collective-permute-start.32 = (bf16[144,1152]{1,0:T(8,128)(2,1)}, bf16[144,1152]{1,0:T(8,128)(2,1)}, u32[]{:S(2)}, u32[]{:S(2)}) collective-permute-start(bf16[144,1152]{1,0:T(8,128)(2,1)} %get-tuple-element.65), channel_id=1, source_target_pairs={{0,1},{1,2},{2,3},{3,0},{4,5},{5,6},{6,7},{7,4},{8,9},{9,10},{10,1... | collective-permute-start | bytes 995336 | tf_op jit(solution)/shard_map/ppermute | solution.py:17
  64.6 72.2 %collective-permute-start.33 = (bf16[144,1152]{1,0:T(8,128)(2,1)}, bf16[144,1152]{1,0:T(8,128)(2,1)}, u32[]{:S(2)}, u32[]{:S(2)}) collective-permute-start(bf16[144,1152]{1,0:T(8,128)(2,1)} %get-tuple-element.65), channel_id=1, source_target_pairs={{0,2},{1,3},{2,0},{3,1},{4,6},{5,7},{6,4},{7,5},{8,10},{9,11},{10,... | collective-permute-start | bytes 995336 | tf_op jit(solution)/shard_map/ppermute | solution.py:17
  73.0 67.0 %collective-permute-start.34 = (bf16[144,1152]{1,0:T(8,128)(2,1)}, bf16[144,1152]{1,0:T(8,128)(2,1)}, u32[]{:S(2)}, u32[]{:S(2)}) collective-permute-start(bf16[144,1152]{1,0:T(8,128)(2,1)} %get-tuple-element.65), channel_id=1, source_target_pairs={{0,3},{1,0},{2,1},{3,2},{4,7},{5,4},{6,5},{7,6},{8,11},{9,8},{10,9... | collective-permute-start | bytes 995336 | tf_op jit(solution)/shard_map/ppermute | solution.py:17
  83.8 71.2 %collective-permute-start.3 = (bf16[256,1152]{1,0:T(8,128)(2,1)}, bf16[256,1152]{1,0:T(8,128)(2,1)}, u32[]{:S(2)}, u32[]{:S(2)}) collective-permute-start(bf16[256,1152]{1,0:T(8,128)(2,1)} %get-tuple-element.67), channel_id=1, source_target_pairs={{0,1},{1,2},{2,3},{3,0},{4,5},{5,6},{6,7},{7,4},{8,9},{9,10},{10,1... | collective-permute-start | bytes 1769480 | tf_op jit(solution)/shard_map/ppermute | solution.py:17
  107.0 49.6 %collective-permute-start.4 = (bf16[256,1152]{1,0:T(8,128)(2,1)}, bf16[256,1152]{1,0:T(8,128)(2,1)}, u32[]{:S(2)}, u32[]{:S(2)}) collective-permute-start(bf16[256,1152]{1,0:T(8,128)(2,1)} %get-tuple-element.67), channel_id=1, source_target_pairs={{0,2},{1,3},{2,0},{3,1},{4,6},{5,7},{6,4},{7,5},{8,10},{9,11},{10,... | collective-permute-start | bytes 1769480 | tf_op jit(solution)/shard_map/ppermute | solution.py:17
  120.2 36.4 %collective-permute-start.5 = (bf16[256,1152]{1,0:T(8,128)(2,1)}, bf16[256,1152]{1,0:T(8,128)(2,1)S(1)}, u32[]{:S(2)}, u32[]{:S(2)}) collective-permute-start(bf16[256,1152]{1,0:T(8,128)(2,1)} %get-tuple-element.67), channel_id=1, source_target_pairs={{0,3},{1,0},{2,1},{3,2},{4,7},{5,4},{6,5},{7,6},{8,11},{9,8},{10,9... | collective-permute-start | bytes 1769480 | tf_op jit(solution)/shard_map/ppermute | solution.py:17
  156.6 27.2 %collective-permute-start.19 = (bf16[4,72,1152]{2,1,0:T(8,128)(2,1)S(1)}, bf16[4,72,1152]{2,1,0:T(8,128)(2,1)S(1)}, u32[]{:S(2)}, u32[]{:S(2)}) collective-permute-start(bf16[4,72,1152]{2,1,0:T(8,128)(2,1)S(1)} %copy-done.41), channel_id=1, source_target_pairs={{0,8},{4,12},{8,0},{12,4},{16,24},{20,28},{24,16},{28,20},{1,9},{5... | collective-permute-start | bytes 1990664 | tf_op jit(solution)/shard_map/ppermute | solution.py:22
  159.9 24.8 %collective-permute-start.48 = (bf16[128,1152]{1,0:T(8,128)(2,1)S(1)}, bf16[128,1152]{1,0:T(8,128)(2,1)S(1)}, u32[]{:S(2)}, u32[]{:S(2)}) collective-permute-start(bf16[128,1152]{1,0:T(8,128)(2,1)S(1)} %slice.401), channel_id=1, source_target_pairs={{0,16},{4,20},{8,24},{12,28},{16,0},{20,4},{24,8},{28,12},{1,17},{... | collective-permute-start | bytes 884744 | tf_op jit(solution)/shard_map/ppermute | solution.py:22
  163.2 26.5 %collective-permute-start.49 = (bf16[128,1152]{1,0:T(8,128)(2,1)S(1)}, bf16[128,1152]{1,0:T(8,128)(2,1)S(1)}, u32[]{:S(2)}, u32[]{:S(2)}) collective-permute-start(bf16[128,1152]{1,0:T(8,128)(2,1)S(1)} %slice.402), channel_id=1, source_target_pairs={{0,8},{4,12},{8,0},{12,4},{16,24},{20,28},{24,16},{28,20},{1,9},{5... | collective-permute-start | bytes 884744 | tf_op jit(solution)/shard_map/ppermute | solution.py:22
  169.6 56.9 %collective-permute-start.45 = (bf16[256,1152]{1,0:T(8,128)(2,1)S(1)}, bf16[256,1152]{1,0:T(8,128)(2,1)}, u32[]{:S(2)}, u32[]{:S(2)}) collective-permute-start(bf16[256,1152]{1,0:T(8,128)(2,1)S(1)} %collective-permute-done.44), channel_id=1, source_target_pairs={{0,4},{4,0},{8,12},{12,8},{16,20},{20,16},{24,28},{28,24},{1,5},{5... | collective-permute-start | bytes 1769480 | tf_op jit(solution)/shard_map/ppermute | solution.py:22
  170.4 58.9 %collective-permute-start.47 = (bf16[256,1152]{1,0:T(8,128)(2,1)S(1)}, bf16[256,1152]{1,0:T(8,128)(2,1)}, u32[]{:S(2)}, u32[]{:S(2)}) collective-permute-start(bf16[256,1152]{1,0:T(8,128)(2,1)S(1)} %collective-permute-done.46), channel_id=1, source_target_pairs={{0,4},{4,0},{8,12},{12,8},{16,20},{20,16},{24,28},{28,24},{1,5},{5... | collective-permute-start | bytes 1769480 | tf_op jit(solution)/shard_map/ppermute | solution.py:22
  184.7 47.1 %collective-permute-start.20 = (bf16[4,72,1152]{2,1,0:T(8,128)(2,1)S(1)}, bf16[4,72,1152]{2,1,0:T(8,128)(2,1)S(1)}, u32[]{:S(2)}, u32[]{:S(2)}) collective-permute-start(bf16[4,72,1152]{2,1,0:T(8,128)(2,1)S(1)} %collective-permute-done.19), channel_id=1, source_target_pairs={{0,4},{4,0},{8,12},{12,8},{16,20},{20,16},{24,28},{28,24},{1,5},{5... | collective-permute-start | bytes 1990664 | tf_op jit(solution)/shard_map/ppermute | solution.py:22
  190.6 57.7 %collective-permute-start.50 = (bf16[256,1152]{1,0:T(8,128)(2,1)}, bf16[256,1152]{1,0:T(8,128)(2,1)}, u32[]{:S(2)}, u32[]{:S(2)}) collective-permute-start(bf16[256,1152]{1,0:T(8,128)(2,1)} %pad_maximum_fusion.7), channel_id=1, source_target_pairs={{0,4},{4,0},{8,12},{12,8},{16,20},{20,16},{24,28},{28,24},{1,5},{5... | collective-permute-start | bytes 1769480 | tf_op jit(solution)/shard_map/ppermute | solution.py:22
  305.9 53.8 %collective-permute-start.105 = (bf16[144,1152]{1,0:T(8,128)(2,1)}, bf16[144,1152]{1,0:T(8,128)(2,1)}, u32[]{:S(2)}, u32[]{:S(2)}) collective-permute-start(bf16[144,1152]{1,0:T(8,128)(2,1)} %get-tuple-element.101), channel_id=1, source_target_pairs={{0,1},{1,2},{2,3},{3,0},{4,5},{5,6},{6,7},{7,4},{8,9},{9,10},{10,1... | collective-permute-start | bytes 995336 | tf_op jit(solution)/shard_map/ppermute | solution.py:17
  305.9 56.8 %collective-permute-start.106 = (bf16[144,1152]{1,0:T(8,128)(2,1)}, bf16[144,1152]{1,0:T(8,128)(2,1)}, u32[]{:S(2)}, u32[]{:S(2)}) collective-permute-start(bf16[144,1152]{1,0:T(8,128)(2,1)} %get-tuple-element.103), channel_id=1, source_target_pairs={{0,2},{1,3},{2,0},{3,1},{4,6},{5,7},{6,4},{7,5},{8,10},{9,11},{10,... | collective-permute-start | bytes 995336 | tf_op jit(solution)/shard_map/ppermute | solution.py:17
  313.4 42.3 %collective-permute-start.95 = (bf16[288,576]{1,0:T(8,128)(2,1)}, bf16[288,576]{1,0:T(8,128)(2,1)}, u32[]{:S(2)}, u32[]{:S(2)}) collective-permute-start(bf16[288,576]{1,0:T(8,128)(2,1)} %get-tuple-element.100), channel_id=1, source_target_pairs={{0,2},{1,3},{2,0},{3,1},{4,6},{5,7},{6,4},{7,5},{8,10},{9,11},{10,... | collective-permute-start | bytes 995336 | tf_op jit(solution)/shard_map/ppermute | solution.py:17
  314.3 41.4 %collective-permute-start.96 = (bf16[288,576]{1,0:T(8,128)(2,1)}, bf16[288,576]{1,0:T(8,128)(2,1)}, u32[]{:S(2)}, u32[]{:S(2)}) collective-permute-start(bf16[288,576]{1,0:T(8,128)(2,1)} %get-tuple-element.99), channel_id=1, source_target_pairs={{0,3},{1,0},{2,1},{3,2},{4,7},{5,4},{6,5},{7,6},{8,11},{9,8},{10,9... | collective-permute-start | bytes 995336 | tf_op jit(solution)/shard_map/ppermute | solution.py:17
  333.8 34.9 %collective-permute-start.107 = (bf16[144,1152]{1,0:T(8,128)(2,1)}, bf16[144,1152]{1,0:T(8,128)(2,1)}, u32[]{:S(2)}, u32[]{:S(2)}) collective-permute-start(bf16[144,1152]{1,0:T(8,128)(2,1)} %get-tuple-element.102), channel_id=1, source_target_pairs={{0,3},{1,0},{2,1},{3,2},{4,7},{5,4},{6,5},{7,6},{8,11},{9,8},{10,9... | collective-permute-start | bytes 995336 | tf_op jit(solution)/shard_map/ppermute | solution.py:17
  362.7 106.0 %collective-permute-start.51 = (bf16[256,1152]{1,0:T(8,128)(2,1)}, bf16[256,1152]{1,0:T(8,128)(2,1)}, u32[]{:S(2)}, u32[]{:S(2)}) collective-permute-start(bf16[256,1152]{1,0:T(8,128)(2,1)} %get-tuple-element.79), channel_id=1, source_target_pairs={{0,4},{4,0},{8,12},{12,8},{16,20},{20,16},{24,28},{28,24},{1,5},{5... | collective-permute-start | bytes 1769480 | tf_op jit(solution)/shard_map/ppermute | solution.py:22
  394.5 77.4 %collective-permute-start.35 = (bf16[256,1152]{1,0:T(8,128)(2,1)}, bf16[256,1152]{1,0:T(8,128)(2,1)}, u32[]{:S(2)}, u32[]{:S(2)}) collective-permute-start(bf16[256,1152]{1,0:T(8,128)(2,1)} %get-tuple-element.83), channel_id=1, source_target_pairs={{0,4},{4,0},{8,12},{12,8},{16,20},{20,16},{24,28},{28,24},{1,5},{5... | collective-permute-start | bytes 1769480 | tf_op jit(solution)/shard_map/ppermute | solution.py:22
  442.8 26.6 %collective-permute-start.55 = (bf16[256,1152]{1,0:T(8,128)(2,1)}, bf16[256,1152]{1,0:T(8,128)(2,1)}, u32[]{:S(2)}, u32[]{:S(2)}) collective-permute-start(bf16[256,1152]{1,0:T(8,128)(2,1)} %pad_maximum_fusion.8), channel_id=1, source_target_pairs={{0,8},{4,12},{8,0},{12,4},{16,24},{20,28},{24,16},{28,20},{1,9},{5... | collective-permute-start | bytes 1769480 | tf_op jit(solution)/shard_map/ppermute | solution.py:22
  556.1 53.7 %collective-permute-start.63 = (bf16[256,1152]{1,0:T(8,128)(2,1)}, bf16[256,1152]{1,0:T(8,128)(2,1)}, u32[]{:S(2)}, u32[]{:S(2)}) collective-permute-start(bf16[256,1152]{1,0:T(8,128)(2,1)} %get-tuple-element.94), channel_id=1, source_target_pairs={{0,2},{1,3},{2,0},{3,1},{4,6},{5,7},{6,4},{7,5},{8,10},{9,11},{10,... | collective-permute-start | bytes 1769480 | tf_op jit(solution)/shard_map/ppermute | solution.py:17
  558.2 51.5 %collective-permute-start.64 = (bf16[256,1152]{1,0:T(8,128)(2,1)}, bf16[256,1152]{1,0:T(8,128)(2,1)}, u32[]{:S(2)}, u32[]{:S(2)}) collective-permute-start(bf16[256,1152]{1,0:T(8,128)(2,1)} %get-tuple-element.93), channel_id=1, source_target_pairs={{0,1},{1,2},{2,3},{3,0},{4,5},{5,6},{6,7},{7,4},{8,9},{9,10},{10,1... | collective-permute-start | bytes 1769480 | tf_op jit(solution)/shard_map/ppermute | solution.py:17
  620.9 44.4 %collective-permute-start.84 = (bf16[4,72,1152]{2,1,0:T(8,128)(2,1)}, bf16[4,72,1152]{2,1,0:T(8,128)(2,1)}, u32[]{:S(2)}, u32[]{:S(2)}) collective-permute-start(bf16[4,72,1152]{2,1,0:T(8,128)(2,1)} %get-tuple-element.76), channel_id=1, source_target_pairs={{0,4},{4,0},{8,12},{12,8},{16,20},{20,16},{24,28},{28,24},{1,5},{5... | collective-permute-start | bytes 1990664 | tf_op jit(solution)/shard_map/ppermute | solution.py:22
  640.3 25.0 %collective-permute-start.86 = (bf16[4,72,1152]{2,1,0:T(8,128)(2,1)S(1)}, bf16[4,72,1152]{2,1,0:T(8,128)(2,1)S(1)}, u32[]{:S(2)}, u32[]{:S(2)}) collective-permute-start(bf16[4,72,1152]{2,1,0:T(8,128)(2,1)S(1)} %fusion.12), channel_id=1, source_target_pairs={{0,8},{4,12},{8,0},{12,4},{16,24},{20,28},{24,16},{28,20},{1,9},{5... | collective-permute-start | bytes 1990664 | tf_op jit(solution)/shard_map/ppermute | solution.py:22
  (182 other events, 2209.7 us)

commit v2 on v1

v2 whole, which is shorter than its diff:
```python
import functools
import math

import jax
import jax.numpy as jnp
from jax import lax
from jax.experimental import pallas as pl
from jax.experimental.pallas import tpu as pltpu
from jax.sharding import Mesh
from jax.sharding import PartitionSpec as P

HEADS = 16
WIDE = ("chip", "core")
F32 = jnp.float32
BF16 = jnp.bfloat16
LANES = 128
ROOT = math.sqrt(2 / math.pi)


def dot(left, right, dims=((1,), (0,))):
    return lax.dot_general(left, right, (dims, ((), ())), preferred_element_type=F32)


def flip(block, axis, bit):
    size = lax.axis_size(axis)
    return lax.ppermute(block, axis, [(i, i ^ bit) for i in range(size)])


def exchange(blocks, axis):
    return lax.all_to_all(blocks, axis, 0, 0, tiled=False)


def share(block, axis):
    return exchange(jnp.broadcast_to(block[None], (lax.axis_size(axis),) + block.shape), axis)


def ring(block, step):
    n = lax.axis_size("narrow")
    return lax.ppermute(block, "narrow", [(i, (i + step) % n) for i in range(n)])


def together(*values):
    return lax.optimization_barrier(values)


def add_up(blocks):
    return sum(blocks[i].astype(F32) for i in range(blocks.shape[0]))


def place(blocks, index_of):
    buffer = jnp.zeros((len(blocks),) + blocks[0].shape, blocks[0].dtype)
    for j, block in enumerate(blocks):
        buffer = lax.dynamic_update_index_in_dim(buffer, block, index_of(j), 0)
    return buffer


def quad_index(r):
    chip = lax.axis_index("chip")
    core = lax.axis_index("core")
    return 2 * ((chip & 1) ^ (r >> 1)) + (core ^ (r & 1))


def quad_gather(block):
    two = flip(block, "chip", 1)
    pair = flip(jnp.stack([block, two]), "core", 1)
    return place([block, pair[0], two, pair[1]], quad_index)


def ring_sum(terms):
    n = lax.axis_size("narrow")
    z = lax.axis_index("narrow")
    total = lax.dynamic_index_in_dim(terms, z, 0, keepdims=False)
    for j in range(1, n):
        total += ring(lax.dynamic_index_in_dim(terms, lax.rem(z + j, n), 0, keepdims=False), j)
    return total


def ring_gather(block):
    n = lax.axis_size("narrow")
    z = lax.axis_index("narrow")
    blocks = [block] + [ring(block, j) for j in range(1, n)]
    return place(blocks, lambda j: lax.rem(z + n - j, n))


def plane_rows(row):
    chips = lax.axis_size("chip")
    p = 2 * lax.axis_index("chip") + lax.axis_index("core")
    own = jnp.stack([row] + [flip(row, "chip", r) for r in range(1, chips)])
    both = jnp.stack([own, flip(own, "core", 1)], axis=1).reshape((2 * chips,) + row.shape)
    return both[jnp.arange(2 * chips) ^ p]


def plane_share(block):
    own = share(block, "chip")
    return own, flip(own, "core", 1)


def chip_sum(terms):
    chip = lax.axis_index("chip")
    total = lax.dynamic_index_in_dim(terms, chip, 0, keepdims=False).astype(F32)
    for r in range(1, lax.axis_size("chip")):
        term = lax.dynamic_index_in_dim(terms, chip ^ r, 0, keepdims=False)
        total += flip(term, "chip", r).astype(F32)
    return total


def core_add(own, other):
    return (own.astype(F32) + flip(other, "core", 1).astype(F32)).astype(BF16)


def call(kernel, args, outs, scratch=(), scalars=0, name=None, micros=1):
    vmem = pl.BlockSpec(memory_space=pltpu.VMEM)
    smem = pl.BlockSpec(memory_space=pltpu.SMEM)
    return pl.pallas_call(
        kernel,
        out_shape=tuple(jax.ShapeDtypeStruct(shape, dtype) for shape, dtype in outs),
        in_specs=[smem if i < scalars else vmem for i in range(len(args))],
        out_specs=tuple(vmem for _ in outs),
        scratch_shapes=[pltpu.VMEM(shape, dtype) for shape, dtype in scratch],
        compiler_params=pltpu.CompilerParams(vmem_limit_bytes=56 << 20),
        cost_estimate=pl.CostEstimate(
            flops=1000000000 * micros, bytes_accessed=3000000 * micros, transcendentals=0
        ),
        name=name,
    )(*args)


def pack_kernel(n, w, p_ref, fc1_ref, fc2_ref, pack_ref):
    shard = fc1_ref.shape[0]
    rows = fc2_ref.shape[0] // w
    full = fc2_ref.shape[0]
    for q in range(w):

        @pl.when(p_ref[0] == q)
        def _(q=q):
            pack_ref[:rows] = fc2_ref[q * rows : (q + 1) * rows]
            pieces = [
                fc1_ref[part : part + rows, a * full + q * rows : a * full + (q + 1) * rows]
                for part in range(0, shard, rows)
                for a in range(n)
            ]
            pack_ref[rows:] = jnp.concatenate(pieces, axis=1)


def qkv_kernel(n, place_ref, w_ref, out_ref):
    sub = out_ref.shape[1]
    cols = out_ref.shape[2] // 3
    width = w_ref.shape[1] // 3
    for q in range(w_ref.shape[0] // sub):

        @pl.when(place_ref[0] == q)
        def _(q=q):
            for a in range(n):
                out_ref[a] = jnp.concatenate(
                    [
                        w_ref[q * sub : (q + 1) * sub, t * width + a * cols : t * width + (a + 1) * cols]
                        for t in range(3)
                    ],
                    axis=1,
                )


def attend_kernel(
    n, heads, scale, unit_ref, mod_ref, w_ref, bias_ref, mixed_ref, proj_ref, lse_ref, wide_ref
):
    image, width = unit_ref.shape
    tokens = image // n
    cols = w_ref.shape[1] // 3
    size = cols // heads
    pad = jnp.zeros((width, LANES - size), BF16)
    pad_row = jnp.zeros((1, LANES - size), F32)
    bias = []
    for t in range(3 * heads):
        wide_ref[:, t * LANES : (t + 1) * LANES] = jnp.concatenate(
            [w_ref[:, t * size : (t + 1) * size], pad], axis=1
        )
        bias += [bias_ref[:, t * size : (t + 1) * size], pad_row]
    bias = jnp.concatenate(bias, axis=1)
    gain = 1.0 + mod_ref[1:2]
    shift = mod_ref[0:1]

    def project(i, carry):
        rows = pl.ds(pl.multiple_of(i * tokens, tokens), tokens)
        first = (unit_ref[rows].astype(F32) * gain + shift).astype(BF16)
        proj_ref[rows] = (dot(first, wide_ref[...]) + bias).astype(BF16)
        return carry

    lax.fori_loop(0, n, project, 0)
    for h in range(heads):
        keys = proj_ref[:, (heads + h) * LANES : (heads + h + 1) * LANES]
        values = proj_ref[:, (2 * heads + h) * LANES : (2 * heads + h + 1) * LANES]
        values_t = values.T

        def block(i, carry, h=h, keys=keys, values_t=values_t):
            rows = pl.ds(pl.multiple_of(i * tokens, tokens), tokens)
            queries = proj_ref[rows, h * LANES : (h + 1) * LANES]
            scores = dot(keys, queries, ((1,), (1,)))
            top = jnp.max(scores, axis=0, keepdims=True)
            grown = jnp.exp((scores - top) * scale)
            total = jnp.sum(grown, axis=0, keepdims=True)
            mixed = dot(values_t, grown.astype(BF16)) / total
            mixed_ref[i, :, h * size : (h + 1) * size] = mixed.T[:, :size].astype(BF16)
            lse_ref[h : h + 1, rows] = top * scale + jnp.log(total)
            return carry

        lax.fori_loop(0, n, block, 0)


def attend_back_kernel(
    n,
    heads,
    scale,
    core_ref,
    proj_ref,
    lse_ref,
    grad_ref,
    mixed_ref,
    unit_ref,
    mod_ref,
    *rest,
):
    terms_own_ref, terms_other_ref, grad_proj, proj_sums_ref, grad_wide, delta_ref, first_low = rest[:7]
    terms, query_acc, terms_low = rest[7:]
    image, width = unit_ref.shape
    tokens = image // n
    cols = grad_ref.shape[2]
    size = cols // heads
    pad = jnp.zeros((tokens, LANES - size), BF16)
    ones = jnp.ones((8, LANES), F32)
    gain = 1.0 + mod_ref[1:2]
    shift = mod_ref[0:1]

    def prepare(i, carry):
        rows = pl.ds(pl.multiple_of(i * tokens, tokens), tokens)
        for h in range(heads):
            grad = jnp.concatenate([grad_ref[i, :, h * size : (h + 1) * size], pad], axis=1)
            mixed = jnp.concatenate([mixed_ref[i, :, h * size : (h + 1) * size], pad], axis=1)
            grad_wide[rows, h * LANES : (h + 1) * LANES] = grad
            both = grad.astype(F32) * mixed.astype(F32)
            delta = lax.dot_general(
                ones, both, (((1,), (1,)), ((), ())),
                preferred_element_type=F32, precision=lax.Precision.HIGHEST,
            )
            delta_ref[h : h + 1, rows] = delta[0:1]
        first_low[rows] = (unit_ref[rows].astype(F32) * gain + shift).astype(BF16)
        return carry

    lax.fori_loop(0, n, prepare, 0)
    for h in range(heads):
        q_at = slice(h * LANES, (h + 1) * LANES)
        k_at = slice((heads + h) * LANES, (heads + h + 1) * LANES)
        v_at = slice((2 * heads + h) * LANES, (2 * heads + h + 1) * LANES)
        query_acc[...] = jnp.zeros_like(query_acc)

        def block(j, carry, h=h, q_at=q_at, k_at=k_at, v_at=v_at):
            rows = pl.ds(pl.multiple_of(j * tokens, tokens), tokens)
            keys = proj_ref[rows, k_at]
            values = proj_ref[rows, v_at]
            queries = proj_ref[:, q_at]
            grads = grad_wide[:, q_at]
            weights = jnp.exp(dot(keys, queries, ((1,), (1,))) * scale - lse_ref[h : h + 1])
            grad_weights = dot(values, grads, ((1,), (1,)))
            grad_scores = (weights * (grad_weights - delta_ref[h : h + 1])).astype(BF16)
            grad_proj[rows, v_at] = dot(weights.astype(BF16), grads).astype(BF16)
            grad_proj[rows, k_at] = (dot(grad_scores, queries) * scale).astype(BF16)
            query_acc[...] += dot(keys.T, grad_scores)
            return carry

        lax.fori_loop(0, n, block, 0)
        grad_proj[:, q_at] = (query_acc[...] * scale).T.astype(BF16)

    proj_sums_ref[...] = jnp.zeros_like(proj_sums_ref)
    for i in range(n):
        block = grad_proj[i * tokens : (i + 1) * tokens].astype(F32)
        proj_sums_ref[0:1] += jnp.sum(block, axis=0, keepdims=True)
    for t in range(3):
        part = dot(
            first_low[...], grad_proj[:, t * heads * LANES : (t + 1) * heads * LANES], ((0,), (0,))
        )
        terms[:, t * cols : (t + 1) * cols] = jnp.concatenate(
            [part[:, h * LANES : h * LANES + size] for h in range(heads)], axis=1
        )
    to_pieces(terms, terms_low, n)
    terms_own_ref[...] = terms_low[core_ref[0]]
    terms_other_ref[...] = terms_low[1 - core_ref[0]]


def to_pieces(terms, low, n):
    _, chips, _, padded, columns = low.shape
    shard = terms.shape[0] // n
    piece = shard // (2 * chips)
    for a in range(n):
        for q in range(2 * chips):
            at = a * shard + q * piece
            block = terms[at : at + piece].astype(BF16)
            if padded > piece:
                block = jnp.concatenate([block, jnp.zeros((padded - piece, columns), BF16)], axis=0)
            low[q % 2, q // 2, a] = block


def wout_kernel(n, core_ref, mixed_ref, grad_ref, own_ref, other_ref, terms, low):
    step = grad_ref.shape[1] // 3
    for t in range(3):
        lanes = slice(t * step, (t + 1) * step)
        terms[:, lanes] = dot(mixed_ref[...], grad_ref[:, lanes], ((0,), (0,)))
    to_pieces(terms, low, n)
    own_ref[...] = low[core_ref[0]]
    other_ref[...] = low[1 - core_ref[0]]


def first_kernel(n, grad_proj, wide_ref, unit_ref, first_ref, sums_ref):
    tokens = unit_ref.shape[0] // n
    sums_ref[...] = jnp.zeros_like(sums_ref)

    def block(i, carry):
        rows = pl.ds(pl.multiple_of(i * tokens, tokens), tokens)
        grad = dot(grad_proj[rows], wide_ref[...], ((1,), (1,)))
        sums_ref[0:1] += jnp.sum(grad, axis=0, keepdims=True)
        sums_ref[1:2] += jnp.sum(grad * unit_ref[rows].astype(F32), axis=0, keepdims=True)
        first_ref[i] = grad.astype(BF16)
        return carry

    lax.fori_loop(0, n, block, 0)


def mlp_kernel(
    n,
    own_ref,
    other_ref,
    two_own_ref,
    two_other_ref,
    pack_ref,
    bias_ref,
    second_own_ref,
    second_other_ref,
    two_sum_own_ref,
    two_sum_other_ref,
    grad_ref,
    bias_grad_ref,
    fc1,
    fc2,
    active_all,
    hidden_all,
    grad_fc1,
):
    chips, tokens, width = own_ref.shape
    rows = pack_ref.shape[1] // 2
    units = n * rows
    halves = width // units
    for a in range(n):
        fc2[a * rows : (a + 1) * rows] = pack_ref[a, :rows]
        for part in range(halves):
            at = (a * halves + part) * rows
            fc1[at : at + rows] = pack_ref[a, rows:, part * units : (part + 1) * units]
    bias_grad_ref[...] = jnp.zeros_like(bias_grad_ref)
    sides = (
        (own_ref, two_own_ref, second_own_ref, two_sum_own_ref),
        (other_ref, two_other_ref, second_other_ref, two_sum_other_ref),
    )
    for side, refs in enumerate(sides):

        def block(i, carry, side=side, refs=refs):
            x_ref, g_ref, second_ref, two_ref = refs
            at = pl.ds(pl.multiple_of((side * chips + i) * tokens, tokens), tokens)
            hidden = dot(x_ref[i], fc1[...]) + bias_ref[...]
            square = hidden * hidden
            inner = ROOT * (hidden + 0.044715 * square * hidden)
            bend = jnp.tanh(inner)
            half = 0.5 * (1.0 + bend)
            active = (hidden * half).astype(BF16)
            slope = half + 0.5 * hidden * (1.0 - bend * bend) * (ROOT * (1.0 + 3 * 0.044715 * square))
            grad = (dot(g_ref[i], fc2[...], ((1,), (1,))) * slope).astype(BF16)
            active_all[at] = active
            hidden_all[at] = grad
            second_ref[i] = dot(grad, fc1[...], ((1,), (1,))).astype(BF16)
            two_ref[i] = dot(active, fc2[...]).astype(BF16)
            bias_grad_ref[0:1] += jnp.sum(grad.astype(F32), axis=0, keepdims=True)
            return carry

        lax.fori_loop(0, chips, block, 0)
    step = width // 3
    half_rows = chips * tokens
    for t in range(3):
        lanes = slice(t * step, (t + 1) * step)
        part = dot(
            active_all[:half_rows], two_own_ref[:, :, lanes].reshape(half_rows, step), ((0,), (0,))
        ) + dot(
            active_all[half_rows:], two_other_ref[:, :, lanes].reshape(half_rows, step), ((0,), (0,))
        )
        for a in range(n):
            grad_ref[a, :rows, lanes] = part[a * rows : (a + 1) * rows].astype(BF16)
        grad_fc1[lanes] = dot(
            own_ref[:, :, lanes].reshape(half_rows, step), hidden_all[:half_rows], ((0,), (0,))
        ) + dot(
            other_ref[:, :, lanes].reshape(half_rows, step), hidden_all[half_rows:], ((0,), (0,))
        )
    for a in range(n):
        grad_ref[a, rows:] = jnp.concatenate(
            [
                grad_fc1[(a * halves + part) * rows : (a * halves + part + 1) * rows].astype(BF16)
                for part in range(halves)
            ],
            axis=1,
        )


def unpack_kernel(n, got_ref, fc1_ref, fc2_ref):
    w, _, width = got_ref.shape
    rows = got_ref.shape[1] // 2
    units = n * rows
    full = w * rows
    for q in range(w):
        fc2_ref[q * rows : (q + 1) * rows] = got_ref[q, :rows].astype(F32)
    for part in range(width // units):
        for a in range(n):
            at = part * units + a * rows
            fc1_ref[part * rows : (part + 1) * rows, a * full : (a + 1) * full] = jnp.concatenate(
                [got_ref[q, rows:, at : at + rows].astype(F32) for q in range(w)], axis=1
            )


def unpack_qkv_kernel(n, core_ref, own_ref, other_ref, out_ref):
    chips = own_ref.shape[0]
    piece = out_ref.shape[0] // (2 * chips)
    cols = own_ref.shape[3] // 3
    for core in range(2):

        @pl.when(core_ref[0] == core)
        def _(core=core):
            for q in range(2 * chips):
                got_ref = own_ref if q % 2 == core else other_ref
                out_ref[q * piece : (q + 1) * piece] = jnp.concatenate(
                    [
                        got_ref[q // 2, a, :piece, t * cols : (t + 1) * cols].astype(F32)
                        for t in range(3)
                        for a in range(n)
                    ],
                    axis=1,
                )


def rows_mean(rows_in):
    return jnp.mean(rows_in, axis=-1, keepdims=True)


def norm_parts(rows_in):
    centered = rows_in - rows_mean(rows_in)
    inv = lax.rsqrt(rows_mean(centered * centered) + 1e-06)
    return centered * inv, inv


def norm_back(unit, inv, grad_unit):
    return inv * (grad_unit - rows_mean(grad_unit) - unit * rows_mean(grad_unit * unit))


def per_device(
    x_input,
    condition,
    counts,
    w_ada,
    b_ada,
    w_qkv,
    qv_bias,
    w_out,
    b_out,
    w_fc1,
    b_fc1,
    w_fc2,
    b_fc2,
    d_out,
):
    n = lax.axis_size("narrow")
    chips = lax.axis_size("chip")
    w = 2 * chips
    z = lax.axis_index("narrow")
    p = 2 * lax.axis_index("chip") + lax.axis_index("core")
    plane = ("chip", "core")
    slot_count, tokens, width = x_input.shape
    x_rows = x_input.reshape(tokens, width)
    heads = HEADS // n
    head_size = width // HEADS
    score_scale = head_size ** (-0.5)
    shard = width // n
    sub = shard // 4
    hidden_dev = w_fc2.shape[0] // w
    hidden_all = n * hidden_dev
    cols = heads * head_size
    image = n * tokens

    living = (counts[0] > 0).astype(F32)

    quad_at = jnp.asarray(quad_index(0), jnp.int32).reshape(1)
    (qkv_to,) = call(
        functools.partial(qkv_kernel, n),
        (quad_at, w_qkv),
        [((n, sub, 3 * cols), BF16)],
        scalars=1,
        name="qkv_to",
        micros=3,
    )

    cond_act, silu_pull = jax.vjp(jax.nn.silu, condition)
    cond_low = cond_act.astype(BF16)
    x_rows, qkv_to = together(x_rows, qkv_to)
    unit_one, inv_one = norm_parts(x_rows)
    unit_low, cond_low = together(unit_one.astype(BF16), cond_low)
    unit_all = lax.all_gather(unit_low, "narrow", axis=0, tiled=True)
    mod_part = dot(cond_low, w_ada)[0] + b_ada.astype(F32)
    small = jnp.concatenate([mod_part] + [v.astype(F32) for v in (qv_bias, b_out, b_fc1, b_fc2)])
    small_all = ring_gather(small)
    ends = [0]
    for piece in (mod_part, qv_bias, b_out, b_fc1, b_fc2):
        ends.append(ends[-1] + piece.shape[0])
    modulation, qv_full, bout_full, bfc1_full, bfc2_full = [
        small_all[:, low:high].reshape(-1) for low, high in zip(ends[:-1], ends[1:])
    ]
    shift_one, scale_one, gate_one, shift_two, scale_two, gate_two = [
        modulation[None, k * width : (k + 1) * width] for k in range(6)
    ]

    qkv_cols = quad_gather(exchange(qkv_to, "narrow"))
    qkv_cols = qkv_cols.transpose(1, 0, 2, 3).reshape(width, 3 * cols)

    (pack,) = call(
        functools.partial(pack_kernel, n, w),
        (jnp.asarray(p, jnp.int32).reshape(1), w_fc1, w_fc2),
        [((2 * hidden_dev, width), BF16)],
        scalars=1,
        name="pack",
        micros=3,
    )

    out_mine = lax.dynamic_slice_in_dim(w_out, quad_index(0) * sub, sub, 0)
    grad_out = living * d_out.reshape(tokens, width)
    grad_two = (gate_two * grad_out).astype(BF16)
    two_own = share(grad_two, "chip")
    unit_all, out_mine, pack = together(unit_all, out_mine, pack)
    out_ring = [out_mine] + [ring(out_mine, j) for j in range(1, n)]

    pack_all = lax.all_gather(pack, "narrow", axis=0, tiled=False)
    bfc1_dev = lax.dynamic_index_in_dim(bfc1_full.reshape(n, w, hidden_dev), p, 1, keepdims=False)
    bfc1_dev = bfc1_dev.reshape(1, hidden_all)

    qv_two = qv_full.reshape(2, n, cols)
    q_bias = lax.dynamic_index_in_dim(qv_two[0], z, 0, keepdims=True)
    v_bias = lax.dynamic_index_in_dim(qv_two[1], z, 0, keepdims=True)
    bias_three = jnp.concatenate([q_bias, jnp.zeros_like(q_bias), v_bias], axis=1)
    wide_cols = 3 * heads * LANES
    mod_one = jnp.concatenate([shift_one, scale_one], axis=0)
    mixed, projected, lse, qkv_wide = call(
        functools.partial(attend_kernel, n, heads, score_scale),
        (unit_all, mod_one, qkv_cols, bias_three),
        [
            ((n, tokens, cols), BF16),
            ((image, wide_cols), BF16),
            ((8, image), F32),
            ((width, wide_cols), BF16),
        ],
        name="attend",
        micros=26,
    )
    mixed, two_own, *out_ring = together(mixed, two_own, *out_ring)
    two_other = flip(two_own, "core", 1)
    mixed_heads = mixed
    out_quad = quad_gather(place(out_ring, lambda j: lax.rem(z + n - j, n)))
    out_all = out_quad.transpose(1, 0, 2, 3).reshape(width, width)
    mixed = exchange(mixed, "narrow")
    mixed, out_all, pack_all = together(mixed, out_all, pack_all)
    mixed_cat = mixed.transpose(1, 0, 2).reshape(tokens, width)

    branch_one = dot(mixed_cat, out_all) + bout_full[None]
    middle = x_rows + gate_one * branch_one
    unit_two, inv_two = norm_parts(middle)
    second_low = (unit_two * (1.0 + scale_two) + shift_two).astype(BF16)

    core_at = jnp.asarray(lax.axis_index("core"), jnp.int32).reshape(1)
    second_own, second_other = plane_share(second_low)
    side = ((chips, tokens, width), BF16)
    second_terms_own, second_terms_other, two_terms_own, two_terms_other, fc_terms, bfc1_terms = call(
        functools.partial(mlp_kernel, n),
        (second_own, second_other, two_own, two_other, pack_all, bfc1_dev),
        [side, side, side, side, ((n, 2 * hidden_dev, width), BF16), ((8, hidden_all), F32)],
        [
            ((width, hidden_all), BF16),
            ((hidden_all, width), BF16),
            ((w * tokens, hidden_all), BF16),
            ((w * tokens, hidden_all), BF16),
            ((width, hidden_all), F32),
        ],
        name="mlp",
        micros=33,
    )
    bfc1_terms = bfc1_terms[0]
    fc_own = lax.psum_scatter(fc_terms, "narrow", scatter_dimension=0, tiled=False)
    grad_second = add_up(exchange(core_add(second_terms_own, second_terms_other), "chip"))
    two_terms = core_add(two_terms_own, two_terms_other)
    grad_second, two_terms = together(grad_second, two_terms)

    bfc2_terms = jnp.sum(grad_two.astype(F32), axis=0)

    grad_shift_two = jnp.sum(grad_second, axis=0)
    grad_scale_two = jnp.sum(grad_second * unit_two, axis=0)
    grad_middle = grad_out + norm_back(unit_two, inv_two, grad_second * (1.0 + scale_two))
    grad_one = (gate_one * grad_middle).astype(BF16)
    grad_gate_one = jnp.sum(grad_middle * branch_one, axis=0)
    bout_terms = jnp.sum(grad_one.astype(F32), axis=0)
    grad_mixed_cat = dot(grad_one, out_all, ((1,), (1,))).astype(BF16).reshape(tokens, n, cols)
    grad_mixed_cat, fc_own, mixed_cat, grad_one = together(
        grad_mixed_cat, fc_own, mixed_cat, grad_one
    )
    fc_all = lax.all_gather(fc_own, plane, axis=0, tiled=False)
    branch_two = chip_sum(two_terms)
    grad_mixed = exchange(grad_mixed_cat.transpose(1, 0, 2), "narrow")
    branch_two = branch_two + bfc2_full[None]
    result = living * (middle + gate_two * branch_two)
    grad_gate_two = jnp.sum(grad_out * branch_two, axis=0)
    piece = shard // w
    padded = -(-piece // 8) * 8
    wout_sides = call(
        functools.partial(wout_kernel, n),
        (core_at, mixed_cat, grad_one),
        [((chips, n, padded, width), BF16)] * 2,
        [((width, width), F32), ((2, chips, n, padded, width), BF16)],
        name="wout_terms",
        scalars=1,
        micros=4,
    )
    wout_low = core_add(*wout_sides)
    grad_mixed, wout_low = together(grad_mixed, wout_low)
    wout_sum = add_up(exchange(wout_low, "chip")).astype(BF16)

    wqkv_side = ((chips, n, padded, 3 * cols), BF16)
    wqkv_own, wqkv_other, grad_projected, projected_sums = call(
        functools.partial(attend_back_kernel, n, heads, score_scale),
        (core_at, projected, lse, grad_mixed, mixed_heads, unit_all, mod_one),
        [wqkv_side, wqkv_side, ((image, wide_cols), BF16), ((8, wide_cols), F32)],
        [
            ((image, heads * LANES), BF16),
            ((8, image), F32),
            ((image, width), BF16),
            ((width, 3 * cols), F32),
            ((LANES, image), F32),
            ((2, chips, n, padded, 3 * cols), BF16),
        ],
        name="attend_back",
        scalars=1,
        micros=28,
    )
    first_terms, one_sums = call(
        functools.partial(first_kernel, n),
        (grad_projected, qkv_wide, unit_all),
        [((n, tokens, width), BF16), ((8, width), F32)],
        name="first_terms",
        micros=10,
    )
    grad_shift_one = one_sums[0]
    grad_scale_one = one_sums[1]
    grad_first = lax.psum_scatter(first_terms, "narrow", scatter_dimension=0, tiled=False)
    grad_first = grad_first.astype(F32)
    grad_input = grad_middle + norm_back(unit_one, inv_one, grad_first * (1.0 + scale_one))

    projected_sums = projected_sums[0].reshape(3, heads, LANES)[:, :, :head_size].reshape(3, cols)

    mod_terms = jnp.concatenate(
        [grad_shift_one, grad_scale_one, grad_gate_one, grad_shift_two, grad_scale_two, grad_gate_two]
    ).reshape(n, -1)
    qv_terms = jnp.zeros((2, n, cols), F32)
    qv_terms = lax.dynamic_update_slice(
        qv_terms, jnp.stack([projected_sums[0], projected_sums[2]])[:, None], (0, z, 0)
    )
    bfc1_wide = lax.dynamic_update_slice(
        jnp.zeros((n, w, hidden_dev), F32), bfc1_terms.reshape(n, 1, hidden_dev), (0, p, 0)
    )
    small_terms = jnp.concatenate(
        [
            mod_terms,
            qv_terms.reshape(n, -1),
            bout_terms.reshape(n, -1),
            bfc1_wide.reshape(n, -1),
            bfc2_terms.reshape(n, -1),
        ],
        axis=1,
    )
    wqkv_low = core_add(wqkv_own, wqkv_other)
    wqkv_sum = add_up(exchange(wqkv_low, "chip")).astype(BF16)
    wqkv_sum, small_terms, wout_sum = together(wqkv_sum, small_terms, wout_sum)
    wqkv_got = exchange(jnp.concatenate([wqkv_sum, wout_sum], axis=2), "narrow")
    wout_own = add_up(wqkv_got[:, :, 3 * cols :]).astype(BF16)
    wqkv_got, fc_all = together(wqkv_got[:, :, : 3 * cols], fc_all)
    small_own = ring_sum(small_terms)
    mod_size = mod_terms.shape[1]
    mod_low = small_own[:mod_size].astype(BF16)
    cond_part = dot(mod_low[None], w_ada, ((1,), (1,)))
    cond_total = jnp.sum(ring_gather(cond_part), axis=0)
    shared = plane_rows(jnp.concatenate([small_own, cond_act[0]]))
    grad_wfc1, grad_wfc2 = call(
        functools.partial(unpack_kernel, n),
        (fc_all,),
        [((shard, n * w * hidden_dev), F32), ((w * hidden_dev, width), F32)],
        name="unpack",
        micros=8,
    )
    wqkv_mine, wqkv_theirs = plane_share(wqkv_got)
    wout_mine, wout_theirs = plane_share(wout_own)
    grad_wout = place([wout_mine, wout_theirs], lambda r: lax.axis_index("core") ^ r)
    grad_wout = grad_wout.transpose(1, 0, 2, 3)[:, :, :piece].reshape(shard, width).astype(F32)
    (grad_wqkv,) = call(
        functools.partial(unpack_qkv_kernel, n),
        (core_at, wqkv_mine, wqkv_theirs),
        [((shard, 3 * width), F32)],
        scalars=1,
        name="unpack_qkv",
        micros=4,
    )
    grad_condition = silu_pull(cond_total)[0]
    mod_rows = shared[:, :mod_size].astype(BF16)
    cond_rows = shared[:, small_own.shape[0] :].astype(BF16)
    grad_wada = dot(cond_rows, mod_rows, ((0,), (0,)))
    grad_bada = jnp.sum(mod_rows.astype(F32), axis=0)
    bias_sums = jnp.sum(shared[:, mod_size : small_own.shape[0]], axis=0)
    ends = [0]
    for piece in (qv_bias, b_out, b_fc1, b_fc2):
        ends.append(ends[-1] + piece.shape[0])
    grad_qv, grad_bout, grad_bfc1, grad_bfc2 = [
        bias_sums[low:high] for low, high in zip(ends[:-1], ends[1:])
    ]
    return (
        result[None],
        grad_input[None],
        grad_condition,
        grad_wada,
        grad_bada,
        grad_wqkv,
        grad_qv,
        grad_wout,
        grad_bout,
        grad_wfc1,
        grad_bfc1,
        grad_wfc2,
        grad_bfc2,
    )


def solution(mesh):
    narrow = mesh.shape["narrow"]
    mesh = Mesh(mesh.devices.reshape(-1, 2, narrow), ("chip", "core", "narrow"))
    in_specs = (
        P(WIDE, "narrow", None),
        P(WIDE, None),
        P(WIDE),
        P(None, "narrow"),
        P("narrow"),
        P("narrow", None),
        P("narrow"),
        P("narrow", None),
        P("narrow"),
        P("narrow", None),
        P("narrow"),
        P("narrow", None),
        P("narrow"),
        P(WIDE, "narrow", None),
    )
    out_specs = (
        P(WIDE, "narrow", None),
        P(WIDE, "narrow", None),
        P(WIDE, None),
        P(None, "narrow"),
        P("narrow"),
        P("narrow", None),
        P("narrow"),
        P("narrow", None),
        P("narrow"),
        P("narrow", None),
        P("narrow"),
        P("narrow", None),
        P("narrow"),
    )
    return jax.shard_map(
        per_device, mesh=mesh, in_specs=in_specs, out_specs=out_specs, check_vma=False
    )
```

time: 738 us -> 514 us (0.70)
  local copies, waits for them, and re-layouts: 165 us -> 41.6 us
  Pallas kernels: 0 us -> 121 us
  matrix products: 108 us -> 17.5 us
  starting transfers between devices: 150 us -> 77.7 us
  waiting for transfers between devices: 233 us -> 197 us
  other arithmetic: 69.2 us -> 37.6 us
  between operations: 3.46 us -> 15.7 us
    ppermute x45 -> x12, waiting for transfers between devices: 143 us -> 1.46 us  [ring(): lax.ppermute(block, 'narrow', [(i, (i + step) % n) for i in range(n)])]
    all_to_all x0 -> x11, waiting for transfers between devices: none -> 129 us  [exchange(): return lax.all_to_all(blocks, axis, 0, 0, tiled=False)]
    pallas_call x0 -> x9, Pallas kernels: none -> 121 us  [call(): pl.pallas_call(kernel, out_shape=tuple((jax.ShapeDtypeStruct(shape, dtype...]
    ppermute x45 -> x12, starting transfers between devices: 104 us -> 19.7 us  [ring(): lax.ppermute(block, 'narrow', [(i, (i + step) % n) for i in range(n)])]
    dot_general x15 -> x5, matrix products: 64.7 us -> 17.5 us  [dot(): lax.dot_general(left, right, (dims, ((), ())), preferred_element_type=F32)]
    all_to_all x0 -> x11, starting transfers between devices: none -> 46.6 us  [exchange(): return lax.all_to_all(blocks, axis, 0, 0, tiled=False)]
    dot_general x6 -> x0, matrix products: 43.4 us -> none  [the longest x1 15.3 us: per_device(): jnp.einsum('qhd,khd->hqk', grad_mixed, values, preferred_element_type=F32)]
    ppermute x71 -> x19, waiting for transfers between devices: 89.5 us -> 54.1 us  [flip(): return lax.ppermute(block, axis, [(i, i ^ bit) for i in range(size)])]
  transfers between devices with their start and end apart: 116 -> 47, of which waited for: 41 -> 20; matrix products, arithmetic and copies ran while one was open for 31% -> 17% of each run, Pallas kernels for 0% -> 8%
where the time goes in v2:
time: 514 us; the launch traced here: 508 us
  waiting for transfers between devices  197 us (38%)
  Pallas kernels  121 us (24%)
  starting transfers between devices  77.7 us (15%)
  local copies, waits for them, and re-layouts  41.6 us (8%)
  other arithmetic  37.6 us (7%)
  matrix products  17.5 us (3%)
  between operations  15.7 us (3%)
    all_to_all x11, waiting for transfers between devices, exchange(): return lax.all_to_all(blocks, axis, 0, 0, tiled=False)  129 us
    pallas_call x9, Pallas kernels, call(): pl.pallas_call(kernel, out_shape=tuple((jax.ShapeDtypeStruct(shape, dtype...  121 us
    ppermute x19, waiting for transfers between devices, flip(): return lax.ppermute(block, axis, [(i, i ^ bit) for i in range(size)])  54.1 us
    all_to_all x11, starting transfers between devices, exchange(): return lax.all_to_all(blocks, axis, 0, 0, tiled=False)  46.6 us
    ppermute x12, starting transfers between devices, ring(): lax.ppermute(block, 'narrow', [(i, (i + step) % n) for i in range(n)])  19.7 us
    dot_general x5, matrix products, dot(): lax.dot_general(left, right, (dims, ((), ())), preferred_element_type=F32)  17.5 us
    convert_element_type x4, other arithmetic, core_add(): return (own.astype(F32) + flip(other, 'core', 1).astype(F32)).astype(BF16)  14.5 us
    dynamic_update_slice x22, local copies, waits for them, and re-layouts, place(): buffer = lax.dynamic_update_index_in_dim(buffer, block, index_of(j), 0)  13.7 us
  transfers between devices with their start and end apart: 47, of which 20 were waited for; matrix products, arithmetic and copies ran while one was open for 17% of the time, Pallas kernels for 8%

profile of v2, /device:TPU:0, one launch (start us, length us, event | category | flops | bytes accessed | tf_op | source)
XLA Modules:
  0.0 507.7 jit_solution(1338771674197073576)
XLA Ops:
  9.9 6.3 %all-to-all-start = ((bf16[4,72,864]{2,1,0:T(8,128)(2,1)}), bf16[4,72,864]{2,1,0:T(8,128)(2,1)S(1)}, u32[]{:S(2)}, u32[]{:S(2)}) async-start(bf16[4,72,864]{2,1,0:T(8,128)(2,1)} %qkv_to.1), calls=%async_computation | async-start | bytes 1032192 | tf_op jit(solution)/shard_map/all_to_all | solution.py:30
  27.8 3.9 pack.1
  36.7 7.3 %collective-permute-done.3 = bf16[4,72,864]{2,1,0:T(8,128)(2,1)} collective-permute-done((bf16[4,72,864]{2,1,0:T(8,128)(2,1)S(1)}, bf16[4,72,864]{2,1,0:T(8,128)(2,1)}, u32[]{:S(2)}, u32[]{:S(2)}) %collective-permute-start.3) | collective-permute-done | bytes 497696 | tf_op jit(solution)/shard_map/ppermute | solution.py:26
  47.9 4.5 all-to-all-start.1
  61.7 9.5 %all-gather.6.cloned.1.call-done.unit_ref = bf16[1024,1152]{1,0:T(8,128)(2,1)} async-done(((bf16[256,1152]{1,0:T(8,128)(2,1)}), bf16[1024,1152]{1,0:T(8,128)(2,1)}) %all-gather.6.cloned.1.call-update) | async-done | bytes 2359312 | tf_op jit(solution)/shard_map/all_gather | solution.py:507
  75.5 26.7 %attend.1 = (bf16[4,256,288]{2,1,0:T(8,128)(2,1)}, bf16[1024,1536]{1,0:T(8,128)(2,1)}, f32[8,1024]{1,0:T(8,128)}, bf16[1152,1536]{1,0:T(8,128)(2,1)}) custom-call(bf16[1024,1152]{1,0:T(8,128)(2,1)} %all-gather.6.cloned.1.call-done.unit_ref, f32[2,1152]{1,0:T(2,128)} %pad_maximum_fusion.6.mod_ref, bf16[1152,864]{1,0:T(8,128)(2,1)} %bitcast.15.w_ref, ...), custom_call_target="tpu_custom_call" | custom-call | flops 25999998976 | bytes 78000000 | tf_op jit(solution)/shard_map/attend/pallas_call | solution.py:114
  104.0 14.3 %collective-permute-done.8 = bf16[4,72,1152]{2,1,0:T(8,128)(2,1)S(1)} collective-permute-done((bf16[4,72,1152]{2,1,0:T(8,128)(2,1)S(1)}, bf16[4,72,1152]{2,1,0:T(8,128)(2,1)S(1)}, u32[]{:S(2)}, u32[]{:S(2)}) %collective-permute-start.8) | collective-permute-done | bytes 663584 | tf_op jit(solution)/shard_map/ppermute | solution.py:26
  133.5 10.9 %all-to-all-done.2 = bf16[4,256,288]{1,2,0:T(8,128)(2,1)S(1)} async-done(((bf16[4,256,288]{1,2,0:T(8,128)(2,1)}), bf16[4,256,288]{1,2,0:T(8,128)(2,1)S(1)}, u32[]{:S(2)}, u32[]{:S(2)}) %all-to-all-start.2) | async-done | bytes 589856 | tf_op jit(solution)/shard_map/all_to_all | solution.py:30
  145.3 4.0 fusion.30
  151.8 4.5 all-to-all-start.3
  156.9 27.6 %all-to-all-done.3.own_ref = bf16[4,256,1152]{2,1,0:T(8,128)(2,1)} async-done(((bf16[4,256,1152]{2,1,0:T(8,128)(2,1)}), bf16[4,256,1152]{2,1,0:T(8,128)(2,1)}, u32[]{:S(2)}, u32[]{:S(2)}) %all-to-all-start.3) | async-done | bytes 2359328 | tf_op jit(solution)/shard_map/all_to_all | solution.py:30
  189.3 33.0 %mlp.1 = (bf16[4,256,1152]{2,1,0:T(8,128)(2,1)}, bf16[4,256,1152]{2,1,0:T(8,128)(2,1)}, bf16[4,256,1152]{2,1,0:T(8,128)(2,1)}, bf16[4,256,1152]{2,1,0:T(8,128)(2...) custom-call(bf16[4,256,1152]{2,1,0:T(8,128)(2,1)} %all-to-all-done.3.own_ref, ...), custom_call_target="tpu_custom_call" | custom-call | flops 32999999488 | bytes 99000000 | tf_op jit(solution)/shard_map/mlp/pallas_call | solution.py:114
  222.8 4.3 collective-permute-done.12
  227.2 4.4 add_convert_fusion.1
  231.6 4.7 all-to-all-start.4
  236.4 4.4 add_convert_fusion
  240.8 23.8 %all-to-all-done.4 = bf16[4,256,1152]{2,1,0:T(8,128)(2,1)} async-done(((bf16[4,256,1152]{2,1,0:T(8,128)(2,1)}), bf16[4,256,1152]{2,1,0:T(8,128)(2,1)}, u32[]{:S(2)}, u32[]{:S(2)}) %all-to-all-start.4) | async-done | bytes 2359328 | tf_op jit(solution)/shard_map/all_to_all | solution.py:30
  271.4 12.2 %collective-permute-done.14 = bf16[256,1152]{1,0:T(8,128)(2,1)S(1)} collective-permute-done((bf16[256,1152]{1,0:T(8,128)(2,1)S(1)}, bf16[256,1152]{1,0:T(8,128)(2,1)S(1)}, u32[]{:S(2)}, u32[]{:S(2)}) %collective-permute-start.14) | collective-permute-done | bytes 589856 | tf_op jit(solution)/shard_map/ppermute | solution.py:26
  283.6 12.1 %collective-permute-done.15 = bf16[256,1152]{1,0:T(8,128)(2,1)S(1)} collective-permute-done((bf16[256,1152]{1,0:T(8,128)(2,1)S(1)}, bf16[256,1152]{1,0:T(8,128)(2,1)S(1)}, u32[]{:S(2)}, u32[]{:S(2)}) %collective-permute-start.15) | collective-permute-done | bytes 589856 | tf_op jit(solution)/shard_map/ppermute | solution.py:26
  304.3 4.1 wout_terms.1
  314.8 13.9 %all-to-all-done.5 = bf16[4,256,288]{1,2,0:T(8,128)(2,1)S(1)} async-done(((bf16[4,256,288]{1,2,0:T(8,128)(2,1)}), bf16[4,256,288]{1,2,0:T(8,128)(2,1)S(1)}, u32[]{:S(2)}, u32[]{:S(2)}) %all-to-all-start.5) | async-done | bytes 589856 | tf_op jit(solution)/shard_map/all_to_all | solution.py:30
  329.9 28.4 %attend_back.1 = (bf16[4,4,40,864]{3,2,1,0:T(8,128)(2,1)}, bf16[4,4,40,864]{3,2,1,0:T(8,128)(2,1)}, bf16[1024,1536]{1,0:T(8,128)(2,1)}, f32[8,1536]{1,0:T(8,128)}) custom-call(s32[1]{0:T(128)} %bitcast.37.core_ref, bf16[1024,1536]{1,0:T(8,128)(2,1)} %get-tuple-element.85.proj_ref, f32[8,1024]{1,0:T(8,128)} %get-tuple-element.86.lse_ref, ...), custom_call_target="tpu_custom_call" | custom-call | flops 28000000000 | bytes 84000000 | tf_op jit(solution)/shard_map/attend_back/pallas_call | solution.py:114
  358.2 10.0 %first_terms.1 = (bf16[4,256,1152]{2,1,0:T(8,128)(2,1)}, f32[8,1152]{1,0:T(8,128)}) custom-call(bf16[1024,1536]{1,0:T(8,128)(2,1)} %get-tuple-element.94.grad_proj, bf16[1152,1536]{1,0:T(8,128)(2,1)} %get-tuple-element.95.wide_ref, bf16[1024,1152]{1,0:T(8,128)(2,1)} %all-gather.6.cloned.1.call-done.unit_ref), custom_call_target="tpu_custom_call" | custom-call | flops 10000000000 | bytes 30000000 | tf_op jit(solution)/shard_map/first_terms/pallas_call | solution.py:114
  377.5 14.1 %all-to-all-done.7 = bf16[4,4,40,1152]{3,2,1,0:T(8,128)(2,1)S(1)} async-done(((bf16[4,4,40,1152]{3,2,1,0:T(8,128)(2,1)}), bf16[4,4,40,1152]{3,2,1,0:T(8,128)(2,1)S(1)}, u32[]{:S(2)}, u32[]{:S(2)}) %all-to-all-start.7) | async-done | bytes 1474592 | tf_op jit(solution)/shard_map/all_to_all | solution.py:30
  391.6 4.5 all-to-all-start.6
  398.1 13.0 %all-to-all-done.6 = bf16[4,4,40,864]{3,2,1,0:T(8,128)(2,1)} async-done(((bf16[4,4,40,864]{3,2,1,0:T(8,128)(2,1)}), bf16[4,4,40,864]{3,2,1,0:T(8,128)(2,1)}, u32[]{:S(2)}, u32[]{:S(2)}) %all-to-all-start.6) | async-done | bytes 1105952 | tf_op jit(solution)/shard_map/all_to_all | solution.py:30
  444.7 4.6 fusion.20
  449.3 6.9 %all-to-all-done.8 = bf16[4,40,2016]{2,1,0:T(8,128)(2,1)S(1)} async-done(((bf16[4,40,2016]{2,1,0:T(8,128)(2,1)}), bf16[4,40,2016]{2,1,0:T(8,128)(2,1)S(1)}, u32[]{:S(2)}, u32[]{:S(2)}) %all-to-all-start.8) | async-done | bytes 645152 | tf_op jit(solution)/shard_map/all_to_all | solution.py:30
  467.5 4.3 all-to-all-start.9
  472.0 15.5 %all-to-all-done.9.own_ref = bf16[4,4,40,864]{3,2,1,0:T(8,128)(2,1)} async-done(((bf16[4,4,40,864]{3,2,1,0:T(8,128)(2,1)}), bf16[4,4,40,864]{3,2,1,0:T(8,128)(2,1)}, u32[]{:S(2)}, u32[]{:S(2)}) %all-to-all-start.9) | async-done | bytes 1105952 | tf_op jit(solution)/shard_map/all_to_all | solution.py:30
  488.8 7.8 %unpack.1 = (f32[288,4608]{1,0:T(8,128)}, f32[1152,1152]{1,0:T(8,128)}) custom-call(bf16[8,288,1152]{2,1,0:T(8,128)(2,1)} %bitcast.153), custom_call_target="tpu_custom_call" | custom-call | flops 8000000000 | bytes 24000000 | tf_op jit(solution)/shard_map/unpack/pallas_call | solution.py:114
  496.6 4.3 unpack_qkv.1
  (290 shorter events, 142.2 us)
Async XLA Ops:
  9.9 21.8 %all-to-all-start = ((bf16[4,72,864]{2,1,0:T(8,128)(2,1)}), bf16[4,72,864]{2,1,0:T(8,128)(2,1)S(1)}, u32[]{:S(2)}, u32[]{:S(2)}) async-start(bf16[4,72,864]{2,1,0:T(8,128)(2,1)} %qkv_to.1), calls=%async_computation | async-start | bytes 1032192 | tf_op jit(solution)/shard_map/all_to_all | solution.py:30
  16.2 55.0 %all-gather.6.cloned.1.call-start = ((), (), s32[]{:S(2)}) async-start(), calls=%async_computation.13 | async-start | bytes 2949120 | tf_op jit(solution)/shard_map/all_gather | solution.py:507
  21.9 13.0 %collective-permute-start = (f32[4032]{0:T(1024)S(1)}, f32[4032]{0:T(1024)S(1)}, u32[]{:S(2)}, u32[]{:S(2)}) collective-permute-start(f32[4032]{0:T(1024)S(1)} %concatenate.21), channel_id=1, source_target_pairs={{0,1},{1,2},{2,3},{3,0},{4,5},{5,6},{6,7},{7,4},{8,9},{9,10},{10,1... | collective-permute-start | bytes 48392 | tf_op jit(solution)/shard_map/ppermute | solution.py:39
  24.0 11.2 %collective-permute-start.1 = (f32[4032]{0:T(1024)S(1)}, f32[4032]{0:T(1024)S(1)}, u32[]{:S(2)}, u32[]{:S(2)}) collective-permute-start(f32[4032]{0:T(1024)S(1)} %concatenate.21), channel_id=1, source_target_pairs={{0,2},{1,3},{2,0},{3,1},{4,6},{5,7},{6,4},{7,5},{8,10},{9,11},{10,... | collective-permute-start | bytes 48392 | tf_op jit(solution)/shard_map/ppermute | solution.py:39
  31.7 12.4 %collective-permute-start.3 = (bf16[4,72,864]{2,1,0:T(8,128)(2,1)S(1)}, bf16[4,72,864]{2,1,0:T(8,128)(2,1)}, u32[]{:S(2)}, u32[]{:S(2)}) collective-permute-start(bf16[4,72,864]{2,1,0:T(8,128)(2,1)S(1)} %all-to-all-done), channel_id=1, source_target_pairs={{0,8},{8,0},{16,24},{24,16},{1,9},{9,1},{17,25},{25,17},{2,10},{10... | collective-permute-start | bytes 1493000 | tf_op jit(solution)/shard_map/ppermute | solution.py:26
  46.2 9.8 %collective-permute-start.4 = (bf16[2,4,72,864]{3,2,1,0:T(8,128)(2,1)}, bf16[2,4,72,864]{3,2,1,0:T(8,128)(2,1)}, u32[]{:S(2)}, u32[]{:S(2)}) collective-permute-start(bf16[2,4,72,864]{3,2,1,0:T(8,128)(2,1)} %pad_maximum_fusion.1), channel_id=1, source_target_pairs={{0,4},{4,0},{1,5},{5,1},{2,6},{6,2},{3,7},{7,3},{8,12},{12,8},{9,1... | collective-permute-start | bytes 2985992 | tf_op jit(solution)/shard_map/ppermute | solution.py:26
  47.9 54.3 %all-to-all-start.1 = ((bf16[4,256,1152]{2,1,0:T(8,128)(2,1)}), bf16[4,256,1152]{2,1,0:T(8,128)(2,1)}, u32[]{:S(2)}, u32[]{:S(2)}) async-start(bf16[4,256,1152]{2,1,0:T(8,128)(2,1)} %broadcast_in_dim.155), calls=%async_computation.1 | async-start | bytes 4718592 | tf_op jit(solution)/shard_map/all_to_all | solution.py:30
  52.4 92.0 %all-gather.8.cloned.1.call-start = ((), (), s32[]{:S(2)}) async-start(), calls=%async_computation.16 | async-start | bytes 3317760 | tf_op jit(solution)/shard_map/all_gather | solution.py:540
  71.2 31.0 %collective-permute-start.5 = (bf16[72,1152]{1,0:T(8,128)(2,1)S(1)}, bf16[72,1152]{1,0:T(8,128)(2,1)S(1)}, u32[]{:S(2)}, u32[]{:S(2)}) collective-permute-start(bf16[72,1152]{1,0:T(8,128)(2,1)S(1)} %copy-done.11), channel_id=1, source_target_pairs={{0,1},{1,2},{2,3},{3,0},{4,5},{5,6},{6,7},{7,4},{8,9},{9,10},{10,1... | collective-permute-start | bytes 497672 | tf_op jit(solution)/shard_map/ppermute | solution.py:39
  71.2 31.0 %collective-permute-start.6 = (bf16[72,1152]{1,0:T(8,128)(2,1)S(1)}, bf16[72,1152]{1,0:T(8,128)(2,1)S(1)}, u32[]{:S(2)}, u32[]{:S(2)}) collective-permute-start(bf16[72,1152]{1,0:T(8,128)(2,1)S(1)} %copy-done.11), channel_id=1, source_target_pairs={{0,2},{1,3},{2,0},{3,1},{4,6},{5,7},{6,4},{7,5},{8,10},{9,11},{10,... | collective-permute-start | bytes 497672 | tf_op jit(solution)/shard_map/ppermute | solution.py:39
  72.8 29.4 %collective-permute-start.7 = (bf16[72,1152]{1,0:T(8,128)(2,1)S(1)}, bf16[72,1152]{1,0:T(8,128)(2,1)S(1)}, u32[]{:S(2)}, u32[]{:S(2)}) collective-permute-start(bf16[72,1152]{1,0:T(8,128)(2,1)S(1)} %copy-done.11), channel_id=1, source_target_pairs={{0,3},{1,0},{2,1},{3,2},{4,7},{5,4},{6,5},{7,6},{8,11},{9,8},{10,9... | collective-permute-start | bytes 497672 | tf_op jit(solution)/shard_map/ppermute | solution.py:39
  102.4 15.9 %collective-permute-start.8 = (bf16[4,72,1152]{2,1,0:T(8,128)(2,1)S(1)}, bf16[4,72,1152]{2,1,0:T(8,128)(2,1)S(1)}, u32[]{:S(2)}, u32[]{:S(2)}) collective-permute-start(bf16[4,72,1152]{2,1,0:T(8,128)(2,1)S(1)} %bitcast_dynamic-update-slice_fusion.4), channel_id=1, source_target_pairs={{0,8},{8,0},{16,24},{24,16},{1,9},{9,1},{17,25},{25,17},{2,10},{10... | collective-permute-start | bytes 1990664 | tf_op jit(solution)/shard_map/ppermute | solution.py:26
  119.5 9.2 %collective-permute-start.9 = (bf16[2,4,72,1152]{3,2,0,1:T(8,128)(2,1)}, bf16[2,4,72,1152]{3,2,0,1:T(8,128)(2,1)}, u32[]{:S(2)}, u32[]{:S(2)}) collective-permute-start(bf16[2,4,72,1152]{3,2,0,1:T(8,128)(2,1)} %pad_maximum_fusion), channel_id=1, source_target_pairs={{0,4},{4,0},{1,5},{5,1},{2,6},{6,2},{3,7},{7,3},{8,12},{12,8},{9,1... | collective-permute-start | bytes 3981320 | tf_op jit(solution)/shard_map/ppermute | solution.py:26
  122.6 21.8 %all-to-all-start.2 = ((bf16[4,256,288]{1,2,0:T(8,128)(2,1)}), bf16[4,256,288]{1,2,0:T(8,128)(2,1)S(1)}, u32[]{:S(2)}, u32[]{:S(2)}) async-start(bf16[4,256,288]{1,2,0:T(8,128)(2,1)} %copy.64), calls=%async_computation.2 | async-start | bytes 1179648 | tf_op jit(solution)/shard_map/all_to_all | solution.py:30
  151.8 32.6 %all-to-all-start.3 = ((bf16[4,256,1152]{2,1,0:T(8,128)(2,1)}), bf16[4,256,1152]{2,1,0:T(8,128)(2,1)}, u32[]{:S(2)}, u32[]{:S(2)}) async-start(bf16[4,256,1152]{2,1,0:T(8,128)(2,1)} %broadcast_in_dim.163), calls=%async_computation.3 | async-start | bytes 4718592 | tf_op jit(solution)/shard_map/all_to_all | solution.py:30
  156.3 146.9 %reduce-scatter.3.cloned.1.call-start = ((), (), s32[]{:S(2)}) async-start(), calls=%async_computation.14 | async-start | bytes 3317760 | tf_op jit(solution)/shard_map/reduce_scatter | solution.py:594
  156.8 29.3 %collective-permute-start.11 = (bf16[4,256,1152]{2,1,0:T(8,128)(2,1)}, bf16[4,256,1152]{2,1,0:T(8,128)(2,1)}, u32[]{:S(2)}, u32[]{:S(2)}) collective-permute-start(bf16[4,256,1152]{2,1,0:T(8,128)(2,1)} %all-to-all-done.1.two_own_ref), channel_id=1, source_target_pairs={{0,4},{4,0},{1,5},{5,1},{2,6},{6,2},{3,7},{7,3},{8,12},{12,8},{9,1... | collective-permute-start | bytes 7077896 | tf_op jit(solution)/shard_map/ppermute | solution.py:26
  222.5 14.0 %collective-permute-start.13 = (bf16[4,256,1152]{2,1,0:T(8,128)(2,1)}, bf16[4,256,1152]{2,1,0:T(8,128)(2,1)}, u32[]{:S(2)}, u32[]{:S(2)}) collective-permute-start(bf16[4,256,1152]{2,1,0:T(8,128)(2,1)} %get-tuple-element.82), channel_id=1, source_target_pairs={{0,4},{4,0},{1,5},{5,1},{2,6},{6,2},{3,7},{7,3},{8,12},{12,8},{9,1... | collective-permute-start | bytes 7077896 | tf_op jit(solution)/shard_map/ppermute | solution.py:26
  231.6 33.1 %all-to-all-start.4 = ((bf16[4,256,1152]{2,1,0:T(8,128)(2,1)}), bf16[4,256,1152]{2,1,0:T(8,128)(2,1)}, u32[]{:S(2)}, u32[]{:S(2)}) async-start(bf16[4,256,1152]{2,1,0:T(8,128)(2,1)} %add_convert_fusion.1), calls=%async_computation.4 | async-start | bytes 4718592 | tf_op jit(solution)/shard_map/all_to_all | solution.py:30
  267.2 16.3 %collective-permute-start.14 = (bf16[256,1152]{1,0:T(8,128)(2,1)S(1)}, bf16[256,1152]{1,0:T(8,128)(2,1)S(1)}, u32[]{:S(2)}, u32[]{:S(2)}) collective-permute-start(bf16[256,1152]{1,0:T(8,128)(2,1)S(1)} %get-tuple-element.132), channel_id=1, source_target_pairs={{0,8},{8,0},{16,24},{24,16},{1,9},{9,1},{17,25},{25,17},{2,10},{10... | collective-permute-start | bytes 1769480 | tf_op jit(solution)/shard_map/ppermute | solution.py:26
  268.7 26.9 %collective-permute-start.15 = (bf16[256,1152]{1,0:T(8,128)(2,1)S(1)}, bf16[256,1152]{1,0:T(8,128)(2,1)S(1)}, u32[]{:S(2)}, u32[]{:S(2)}) collective-permute-start(bf16[256,1152]{1,0:T(8,128)(2,1)S(1)} %get-tuple-element.134), channel_id=1, source_target_pairs={{0,16},{8,24},{16,0},{24,8},{1,17},{9,25},{17,1},{25,9},{2,18},{10... | collective-permute-start | bytes 1769480 | tf_op jit(solution)/shard_map/ppermute | solution.py:26
  269.3 26.4 %collective-permute-start.16 = (bf16[256,1152]{1,0:T(8,128)(2,1)S(1)}, bf16[256,1152]{1,0:T(8,128)(2,1)S(1)}, u32[]{:S(2)}, u32[]{:S(2)}) collective-permute-start(bf16[256,1152]{1,0:T(8,128)(2,1)S(1)} %get-tuple-element.133), channel_id=1, source_target_pairs={{0,24},{8,16},{16,8},{24,0},{1,25},{9,17},{17,9},{25,1},{2,26},{10... | collective-permute-start | bytes 1769480 | tf_op jit(solution)/shard_map/ppermute | solution.py:26
  308.4 20.3 %all-to-all-start.5 = ((bf16[4,256,288]{1,2,0:T(8,128)(2,1)}), bf16[4,256,288]{1,2,0:T(8,128)(2,1)S(1)}, u32[]{:S(2)}, u32[]{:S(2)}) async-start(bf16[4,256,288]{1,2,0:T(8,128)(2,1)} %bitcast.41), calls=%async_computation.6 | async-start | bytes 1179648 | tf_op jit(solution)/shard_map/all_to_all | solution.py:30
  311.9 102.8 %reduce-scatter.5.cloned.1.call-start = ((), (), s32[]{:S(2)}) async-start(), calls=%async_computation.15 | async-start | bytes 2949120 | tf_op jit(solution)/shard_map/reduce_scatter | solution.py:658
  368.3 98.2 %all-gather.10.cloned.1.call-start = ((), (), s32[]{:S(2)}) async-start(), calls=%async_computation.17 | async-start | bytes 5971968 | tf_op jit(solution)/shard_map/all_gather | solution.py:611
  368.9 22.7 %all-to-all-start.7 = ((bf16[4,4,40,1152]{3,2,1,0:T(8,128)(2,1)}), bf16[4,4,40,1152]{3,2,1,0:T(8,128)(2,1)S(1)}, u32[]{:S(2)}, u32[]{:S(2)}) async-start(bf16[4,4,40,1152]{3,2,1,0:T(8,128)(2,1)} %add_convert_fusion.2), calls=%async_computation.9 | async-start | bytes 2949120 | tf_op jit(solution)/shard_map/all_to_all | solution.py:30
  391.6 19.5 %all-to-all-start.6 = ((bf16[4,4,40,864]{3,2,1,0:T(8,128)(2,1)}), bf16[4,4,40,864]{3,2,1,0:T(8,128)(2,1)}, u32[]{:S(2)}, u32[]{:S(2)}) async-start(bf16[4,4,40,864]{3,2,1,0:T(8,128)(2,1)} %add_convert_fusion.3), calls=%async_computation.8 | async-start | bytes 2293760 | tf_op jit(solution)/shard_map/all_to_all | solution.py:30
  430.6 11.5 %collective-permute-start.25 = (f32[5184]{0:T(1024)S(1)}, f32[5184]{0:T(1024)S(1)}, u32[]{:S(2)}, u32[]{:S(2)}) collective-permute-start(f32[5184]{0:T(1024)S(1)} %pad_maximum_fusion.5), channel_id=1, source_target_pairs={{0,8},{8,0},{16,24},{24,16},{1,9},{9,1},{17,25},{25,17},{2,10},{10... | collective-permute-start | bytes 62216 | tf_op jit(solution)/shard_map/ppermute | solution.py:26
  432.1 10.0 %collective-permute-start.26 = (f32[5184]{0:T(1024)S(1)}, f32[5184]{0:T(1024)S(1)}, u32[]{:S(2)}, u32[]{:S(2)}) collective-permute-start(f32[5184]{0:T(1024)S(1)} %pad_maximum_fusion.5), channel_id=1, source_target_pairs={{0,16},{8,24},{16,0},{24,8},{1,17},{9,25},{17,1},{25,9},{2,18},{10... | collective-permute-start | bytes 62216 | tf_op jit(solution)/shard_map/ppermute | solution.py:26
  438.0 18.2 %all-to-all-start.8 = ((bf16[4,40,2016]{2,1,0:T(8,128)(2,1)}), bf16[4,40,2016]{2,1,0:T(8,128)(2,1)S(1)}, u32[]{:S(2)}, u32[]{:S(2)}) async-start(bf16[4,40,2016]{2,1,0:T(8,128)(2,1)} %pad_maximum_fusion.2), calls=%async_computation.10 | async-start | bytes 1310720 | tf_op jit(solution)/shard_map/all_to_all | solution.py:30
  457.1 9.4 %all-to-all-start.10 = ((bf16[4,40,1152]{2,1,0:T(8,128)(2,1)}), bf16[4,40,1152]{2,1,0:T(8,128)(2,1)S(1)}, u32[]{:S(2)}, u32[]{:S(2)}) async-start(bf16[4,40,1152]{2,1,0:T(8,128)(2,1)} %broadcast_in_dim.177), calls=%async_computation.12 | async-start | bytes 737280 | tf_op jit(solution)/shard_map/all_to_all | solution.py:30
  467.5 20.0 %all-to-all-start.9 = ((bf16[4,4,40,864]{3,2,1,0:T(8,128)(2,1)}), bf16[4,4,40,864]{3,2,1,0:T(8,128)(2,1)}, u32[]{:S(2)}, u32[]{:S(2)}) async-start(bf16[4,4,40,864]{3,2,1,0:T(8,128)(2,1)} %broadcast_in_dim.174), calls=%async_computation.11 | async-start | bytes 2293760 | tf_op jit(solution)/shard_map/all_to_all | solution.py:30
  (47 other events, 334.1 us)
Sparse Core Ops, SparseCore 0:
  19.2 51.9 all-gather.5
  75.6 60.9 all-gather.7
  223.0 50.6 reduce-scatter.2
  368.4 46.2 reduce-scatter.4
  416.4 41.6 all-gather.9
